TPU v7x, 32 devices: a whole 2x2x4 slice. The times are simulated.
32 devices in a mesh: ctx: 8 (over y, x, core), wsh: 4 (over z).
Axes of the slice: x: 2, y: 2, z: 4, core: 2. Of those that a mesh axis runs over, the one named last changes fastest.
Arguments:
- tokens: bfloat16 [4, 2048, 1088], P('wsh', 'ctx'), may hold values from -6 to 6
- seq_lengths: int32 [4, 5], P('wsh'), may hold values from 96 to 1280, as said below
- cotangent: bfloat16 [4, 2048, 1088], P('wsh', 'ctx'), may hold values from -6 to 6
- ln1_gain: bfloat16 [1088], P('wsh'), may hold values from 0.5 to 1.5
- ln1_bias: bfloat16 [1088], P('wsh'), may hold values from -1.25 to 1.25
- w_qkv: bfloat16 [1088, 3264], P('wsh'), may hold values from -0.1875 to 0.1875
- b_query: bfloat16 [1088], P('wsh'), may hold values from -1.75 to 1.75
- b_value: bfloat16 [1088], P('wsh'), may hold values from -0.625 to 0.625
- w_out: bfloat16 [1088, 1088], P('wsh'), may hold values from -0.375 to 0.375
- b_out: bfloat16 [1088], P('wsh'), may hold values from -1.25 to 1.25
- ln2_gain: bfloat16 [1088], P('wsh'), may hold values from 0.5 to 1.5
- ln2_bias: bfloat16 [1088], P('wsh'), may hold values from -1.25 to 1.25
- w_up: bfloat16 [1088, 4352], P('wsh'), may hold values from -0.1875 to 0.1875
- b_up: bfloat16 [4352], P('wsh'), may hold values from -1.75 to 1.75
- w_down: bfloat16 [4352, 1088], P('wsh'), may hold values from -0.09375 to 0.09375
- b_down: bfloat16 [1088], P('wsh'), may hold values from -1.25 to 1.25
Outputs:
- output: bfloat16 [4, 2048, 1088], P('wsh', 'ctx')
- grad_tokens: float32 [4, 2048, 1088], P('wsh', 'ctx')
- grad_ln1_gain: float32 [1088], P('wsh')
- grad_ln1_bias: float32 [1088], P('wsh')
- grad_w_qkv: float32 [1088, 3264], P('wsh')
- grad_b_query: float32 [1088], P('wsh')
- grad_b_value: float32 [1088], P('wsh')
- grad_w_out: float32 [1088, 1088], P('wsh')
- grad_b_out: float32 [1088], P('wsh')
- grad_ln2_gain: float32 [1088], P('wsh')
- grad_ln2_bias: float32 [1088], P('wsh')
- grad_w_up: float32 [1088, 4352], P('wsh')
- grad_b_up: float32 [4352], P('wsh')
- grad_w_down: float32 [4352, 1088], P('wsh')
- grad_b_down: float32 [1088], P('wsh')
Inputs may be any that keep to these rules, and one draw needn't show every extreme that they name: seq_lengths[g] holds group g's prompt length first, then the lengths of its 4 continuations, all positive; they sum to 2048 and the prompt is the longest.
All inputs are finite; a program needn't handle non-finite values.
Results may differ from a plain program's by a relative error of at most 0.018.
Values may be sent and summed in bfloat16 or wider, within the bound.
A program may use at most 320 MiB of HBM per device.

v0:
```python
import math

import jax
import jax.numpy as jnp
from jax import lax
from jax.sharding import PartitionSpec as P

D = 1088
HEADS = 17
HEAD_DIM = 64


def normalize(inputs):
    center = inputs - jnp.mean(inputs, -1, keepdims=True)
    inverse = lax.rsqrt(jnp.mean(center * center, -1, keepdims=True) + 1e-05)
    return (center * inverse, inverse)


def norm_back(grad_in, normed, inverse, gain):
    scaled = grad_in * gain
    return inverse * (
        scaled
        - jnp.mean(scaled, -1, keepdims=True)
        - normed * jnp.mean(scaled * normed, -1, keepdims=True)
    )


def rows_product(left, right):
    return lax.dot_general(
        left, right, (((0,), (0,)), ((), ())), preferred_element_type=jnp.float32
    )


def cols_product(left, right):
    return lax.dot_general(
        left, right, (((1,), (1,)), ((), ())), preferred_element_type=jnp.float32
    )


def sequence_ids(lengths, positions):
    bounds = jnp.cumsum(lengths)
    return jnp.sum((positions[:, None] >= bounds[None, :]).astype(jnp.int32), axis=1)


def allowed_pairs(lengths, query_pos, key_pos):
    query_owner = sequence_ids(lengths, query_pos)
    key_owner = sequence_ids(lengths, key_pos)
    return (key_pos[None, :] <= query_pos[:, None]) & (
        (key_owner[None, :] == 0) | (key_owner[None, :] == query_owner[:, None])
    )


def over_blocks(state_in, arrays, step_fn):
    total_rows = arrays[0].shape[0]
    block_rows = math.gcd(total_rows, 512)

    def advance(block_index, state_now):
        offset = block_index * block_rows
        pieces = tuple((lax.dynamic_slice_in_dim(array, offset, block_rows, 0) for array in arrays))
        return step_fn(state_now, pieces, offset)

    return lax.fori_loop(0, total_rows // block_rows, advance, state_in)


def sectioned_sum(partials):
    shares = lax.psum_scatter(partials, "wsh", scatter_dimension=0, tiled=True)
    return lax.psum(shares, "ctx")


def on_device(
    tokens,
    seq_lengths,
    cotangent,
    ln1_gain,
    ln1_bias,
    w_qkv,
    b_query,
    b_value,
    w_out,
    b_out,
    ln2_gain,
    ln2_bias,
    w_up,
    b_up,
    w_down,
    b_down,
):
    token_rows, grad_rows = (tokens[0], cotangent[0])
    shards = (
        w_qkv,
        w_out,
        w_up,
        w_down,
        b_query,
        b_value,
        b_out,
        b_up,
        b_down,
        ln1_gain,
        ln1_bias,
        ln2_gain,
        ln2_bias,
    )
    gathered = (
        lax.all_gather(shards[0], "wsh", axis=0, tiled=True),
        lax.all_gather(shards[1], "wsh", axis=0, tiled=True),
        lax.all_gather(shards[2], "wsh", axis=0, tiled=True),
        lax.all_gather(shards[3], "wsh", axis=0, tiled=True),
        lax.all_gather(shards[4], "wsh", axis=0, tiled=True),
        lax.all_gather(shards[5], "wsh", axis=0, tiled=True),
        lax.all_gather(shards[6], "wsh", axis=0, tiled=True),
        lax.all_gather(shards[7], "wsh", axis=0, tiled=True),
        lax.all_gather(shards[8], "wsh", axis=0, tiled=True),
        lax.all_gather(shards[9], "wsh", axis=0, tiled=True),
        lax.all_gather(shards[10], "wsh", axis=0, tiled=True),
        lax.all_gather(shards[11], "wsh", axis=0, tiled=True),
        lax.all_gather(shards[12], "wsh", axis=0, tiled=True),
    )
    qkv_full, out_full, up_full, down_full = (gathered[0], gathered[1], gathered[2], gathered[3])
    query_bias, value_bias, out_bias, up_bias, down_bias = [
        piece.astype(jnp.float32) for piece in gathered[4:9]
    ]
    gain_one, shift_one, gain_two, shift_two = [
        piece.astype(jnp.float32) for piece in gathered[9:13]
    ]
    lengths = seq_lengths[0]
    tok_rows = token_rows.shape[0]
    my_pos = lax.axis_index("ctx") * tok_rows + jnp.arange(tok_rows, dtype=jnp.int32)
    scale_qk = HEAD_DIM ** (-0.5)
    inputs = token_rows.astype(jnp.float32)
    normed_one, inverse_one = normalize(inputs)
    hidden_one = (normed_one * gain_one + shift_one).astype(jnp.bfloat16)
    joint_proj = jnp.dot(hidden_one, qkv_full, preferred_element_type=jnp.float32)
    queries = (joint_proj[:, :D] + query_bias).astype(jnp.bfloat16)
    key_rows = joint_proj[:, D : 2 * D].astype(jnp.bfloat16)
    value_rows = (joint_proj[:, 2 * D :] + value_bias).astype(jnp.bfloat16)
    query_heads = queries.reshape(tok_rows, HEADS, HEAD_DIM)
    my_key_heads = key_rows.reshape(tok_rows, HEADS, HEAD_DIM)
    my_value_heads = value_rows.reshape(tok_rows, HEADS, HEAD_DIM)

    def forward_step(state_now, pieces, first_row):
        key_heads = pieces[0].reshape(-1, HEADS, HEAD_DIM)
        value_heads = pieces[1].reshape(-1, HEADS, HEAD_DIM)
        key_pos = first_row + jnp.arange(key_heads.shape[0], dtype=jnp.int32)
        allowed = allowed_pairs(lengths, my_pos, key_pos)

        def forward_compute(inner):
            peak_old, total_old, accum_old = inner
            scores = (
                jnp.einsum(
                    "qhd,khd->hqk", query_heads, key_heads, preferred_element_type=jnp.float32
                )
                * scale_qk
            )
            scores = jnp.where(allowed[None], scores, -1e30)
            peak_new = jnp.maximum(peak_old, jnp.max(scores, -1))
            factor = jnp.exp(peak_old - peak_new)
            expos = jnp.where(allowed[None], jnp.exp(scores - peak_new[:, :, None]), 0.0)
            total_new = total_old * factor + jnp.sum(expos, -1)
            accum_new = accum_old * factor.T[:, :, None] + jnp.einsum(
                "hqk,khd->qhd",
                expos.astype(jnp.bfloat16),
                value_heads,
                preferred_element_type=jnp.float32,
            )
            return (peak_new, total_new, accum_new)

        return lax.cond(jnp.any(allowed), forward_compute, lambda inner: inner, state_now)

    start_state = (
        jnp.full((HEADS, tok_rows), -1e30, jnp.float32),
        jnp.zeros((HEADS, tok_rows), jnp.float32),
        jnp.zeros((tok_rows, HEADS, HEAD_DIM), jnp.float32),
    )
    peak, total, accum = over_blocks(
        start_state,
        (
            lax.all_gather(key_rows, "ctx", axis=0, tiled=True),
            lax.all_gather(value_rows, "ctx", axis=0, tiled=True),
        ),
        forward_step,
    )
    mixed = accum / total.T[:, :, None]
    log_sum = (peak + jnp.log(total)).T
    mixed_low = mixed.reshape(tok_rows, D).astype(jnp.bfloat16)
    middle = inputs + jnp.dot(mixed_low, out_full, preferred_element_type=jnp.float32) + out_bias
    normed_two, inverse_two = normalize(middle)
    hidden_two = (normed_two * gain_two + shift_two).astype(jnp.bfloat16)
    pre_act = jnp.dot(hidden_two, up_full, preferred_element_type=jnp.float32) + up_bias
    activ_low = jax.nn.gelu(pre_act, approximate=False).astype(jnp.bfloat16)
    result = middle + jnp.dot(activ_low, down_full, preferred_element_type=jnp.float32) + down_bias
    output_rows = result.astype(jnp.bfloat16)
    grad_top_f = grad_rows.astype(jnp.float32)
    grad_down = rows_product(activ_low, grad_rows)
    grad_down_bias = jnp.sum(grad_top_f, 0)
    grad_act = cols_product(grad_rows, down_full)
    cdf_part = 0.5 * (1.0 + lax.erf(pre_act * math.sqrt(0.5)))
    pdf_part = jnp.exp(-0.5 * pre_act * pre_act) / math.sqrt(2.0 * math.pi)
    grad_pre = (grad_act * (cdf_part + pre_act * pdf_part)).astype(jnp.bfloat16)
    grad_up = rows_product(hidden_two, grad_pre)
    grad_up_bias = jnp.sum(grad_pre.astype(jnp.float32), 0)
    grad_h2 = cols_product(grad_pre, up_full)
    grad_gain_two = jnp.sum(grad_h2 * normed_two, 0)
    grad_shift_two = jnp.sum(grad_h2, 0)
    grad_mid = grad_top_f + norm_back(grad_h2, normed_two, inverse_two, gain_two)
    grad_mid_low = grad_mid.astype(jnp.bfloat16)
    grad_out_w = rows_product(mixed_low, grad_mid_low)
    grad_out_bias = jnp.sum(grad_mid_low.astype(jnp.float32), 0)
    grad_mixed = cols_product(grad_mid_low, out_full).astype(jnp.bfloat16)
    grad_heads = grad_mixed.reshape(tok_rows, HEADS, HEAD_DIM)
    delta = jnp.sum(grad_heads.astype(jnp.float32) * mixed, -1)
    lse_all, delta_all = (
        lax.all_gather(log_sum, "ctx", axis=0, tiled=True),
        lax.all_gather(delta, "ctx", axis=0, tiled=True),
    )

    def query_step(state_now, pieces, first_row):
        key_heads = pieces[0].reshape(-1, HEADS, HEAD_DIM)
        value_heads = pieces[1].reshape(-1, HEADS, HEAD_DIM)
        key_pos = first_row + jnp.arange(key_heads.shape[0], dtype=jnp.int32)
        allowed = allowed_pairs(lengths, my_pos, key_pos)

        def query_compute(accum_old):
            scores = (
                jnp.einsum(
                    "qhd,khd->hqk", query_heads, key_heads, preferred_element_type=jnp.float32
                )
                * scale_qk
            )
            probs = jnp.where(allowed[None], jnp.exp(scores - log_sum.T[:, :, None]), 0.0)
            grad_probs = jnp.einsum(
                "qhd,khd->hqk", grad_heads, value_heads, preferred_element_type=jnp.float32
            )
            grad_scores = (probs * (grad_probs - delta.T[:, :, None])).astype(jnp.bfloat16)
            return accum_old + jnp.einsum(
                "hqk,khd->qhd", grad_scores, key_heads, preferred_element_type=jnp.float32
            )

        return lax.cond(jnp.any(allowed), query_compute, lambda inner: inner, state_now)

    zero_heads = jnp.zeros((tok_rows, HEADS, HEAD_DIM), jnp.float32)
    grad_query = over_blocks(
        zero_heads,
        (
            lax.all_gather(key_rows, "ctx", axis=0, tiled=True),
            lax.all_gather(value_rows, "ctx", axis=0, tiled=True),
        ),
        query_step,
    )

    def key_step(state_now, pieces, first_row):
        other_queries = pieces[0].reshape(-1, HEADS, HEAD_DIM)
        other_grads = pieces[1].reshape(-1, HEADS, HEAD_DIM)
        other_count = other_queries.shape[0]
        other_pos = first_row + jnp.arange(other_count, dtype=jnp.int32)
        other_lse = lax.dynamic_slice_in_dim(lse_all, first_row, other_count, 0)
        other_delta = lax.dynamic_slice_in_dim(delta_all, first_row, other_count, 0)
        allowed = allowed_pairs(lengths, other_pos, my_pos)

        def key_compute(inner):
            grad_key_old, grad_value_old = inner
            scores = (
                jnp.einsum(
                    "qhd,khd->hqk", other_queries, my_key_heads, preferred_element_type=jnp.float32
                )
                * scale_qk
            )
            probs = jnp.where(allowed[None], jnp.exp(scores - other_lse.T[:, :, None]), 0.0)
            grad_value_new = grad_value_old + jnp.einsum(
                "hqk,qhd->khd",
                probs.astype(jnp.bfloat16),
                other_grads,
                preferred_element_type=jnp.float32,
            )
            grad_probs = jnp.einsum(
                "qhd,khd->hqk", other_grads, my_value_heads, preferred_element_type=jnp.float32
            )
            grad_scores = (probs * (grad_probs - other_delta.T[:, :, None])).astype(jnp.bfloat16)
            grad_key_new = grad_key_old + jnp.einsum(
                "hqk,qhd->khd", grad_scores, other_queries, preferred_element_type=jnp.float32
            )
            return (grad_key_new, grad_value_new)

        return lax.cond(jnp.any(allowed), key_compute, lambda inner: inner, state_now)

    grad_key, grad_value = over_blocks(
        (zero_heads, zero_heads),
        (
            lax.all_gather(queries, "ctx", axis=0, tiled=True),
            lax.all_gather(grad_mixed, "ctx", axis=0, tiled=True),
        ),
        key_step,
    )
    grad_joint = jnp.concatenate(
        [
            (grad_query * scale_qk).reshape(tok_rows, D),
            (grad_key * scale_qk).reshape(tok_rows, D),
            grad_value.reshape(tok_rows, D),
        ],
        axis=1,
    ).astype(jnp.bfloat16)
    grad_qkv_w = rows_product(hidden_one, grad_joint)
    grad_joint_f = grad_joint.astype(jnp.float32)
    grad_query_bias = jnp.sum(grad_joint_f[:, :D], 0)
    grad_value_bias = jnp.sum(grad_joint_f[:, 2 * D :], 0)
    grad_h1 = cols_product(grad_joint, qkv_full)
    grad_gain_one = jnp.sum(grad_h1 * normed_one, 0)
    grad_shift_one = jnp.sum(grad_h1, 0)
    grad_input = grad_mid + norm_back(grad_h1, normed_one, inverse_one, gain_one)
    matrices = (grad_qkv_w, grad_out_w, grad_up, grad_down)
    vectors = (
        grad_query_bias,
        grad_value_bias,
        grad_out_bias,
        grad_up_bias,
        grad_down_bias,
        grad_gain_one,
        grad_shift_one,
        grad_gain_two,
        grad_shift_two,
    )
    totals = sectioned_sum(matrices + vectors)
    return (
        output_rows[None],
        grad_input[None],
        totals[9],
        totals[10],
        totals[0],
        totals[4],
        totals[5],
        totals[1],
        totals[6],
        totals[11],
        totals[12],
        totals[2],
        totals[7],
        totals[3],
        totals[8],
    )


def solution(mesh):
    in_specs = (
        P("wsh", "ctx", None),
        P("wsh", None),
        P("wsh", "ctx", None),
        P("wsh"),
        P("wsh"),
        P("wsh", None),
        P("wsh"),
        P("wsh"),
        P("wsh", None),
        P("wsh"),
        P("wsh"),
        P("wsh"),
        P("wsh", None),
        P("wsh"),
        P("wsh", None),
        P("wsh"),
    )
    out_specs = (
        P("wsh", "ctx", None),
        P("wsh", "ctx", None),
        P("wsh"),
        P("wsh"),
        P("wsh", None),
        P("wsh"),
        P("wsh"),
        P("wsh", None),
        P("wsh"),
        P("wsh"),
        P("wsh"),
        P("wsh", None),
        P("wsh"),
        P("wsh", None),
        P("wsh"),
    )
    return jax.shard_map(
        on_device, mesh=mesh, in_specs=in_specs, out_specs=out_specs, check_vma=False
    )
```

profile of v0, /device:TPU:0, one launch (start us, length us, event | category | flops | bytes accessed | tf_op | source)
XLA Modules:
  0.0 1941.6 jit_solution(5933484125573785426)
XLA Ops:
  18.5 29.3 %all-reduce.21 = (bf16[1088]{0:T(1024)(128)(2,1)S(1)}, bf16[1088]{0:T(1024)(128)(2,1)S(1)}, bf16[1088]{0:T(1024)(128)(2,1)S(1)}, bf16[1088]{0:T(1024)(128)(2,1)S...) all-reduce(bf16[1088]{0:T(1024)(128)(2,1)S(1)} %dynamic-update-slic, ...), channel_id=1, replica_groups=mesh['ctx'=8,'wsh'=4] {'wsh'}, use_global_device_ids=true, to_apply=%add.1 | all-reduce | flops 13056 | bytes 52224
  49.3 95.3 %all-gather.9.cloned.1.call-done = bf16[1088,3264]{1,0:T(8,128)(2,1)} async-done(((bf16[272,3264]{1,0:T(8,128)(2,1)}), bf16[1088,3264]{1,0:T(8,128)(2,1)}) %all-gather.9.cloned.1.call-update) | async-done | bytes 7102480 | tf_op jit(solution)/shard_map/all_gather | solution.py:105
  159.8 31.1 %all-gather.11.cloned.1.call-done = bf16[2048,1088]{0,1:T(8,128)(2,1)} async-done(((bf16[256,1088]{0,1:T(8,128)(2,1)}), bf16[2048,1088]{0,1:T(8,128)(2,1)}) %all-gather.11.cloned.1.call-update) | async-done | bytes 4456464 | tf_op jit(solution)/shard_map/all_gather | solution.py:178
  190.9 40.4 %all-gather.13.cloned.1.call-done = bf16[2048,1088]{0,1:T(8,128)(2,1)} async-done(((bf16[256,1088]{0,1:T(8,128)(2,1)}), bf16[2048,1088]{0,1:T(8,128)(2,1)}) %all-gather.13.cloned.1.call-update) | async-done | bytes 4456464 | tf_op jit(solution)/shard_map/all_gather | solution.py:179
  231.4 15.2 while.57
  247.5 38.1 %all-gather.15.cloned.1.call-done = bf16[1088,1088]{1,0:T(8,128)(2,1)} async-done(((bf16[272,1088]{1,0:T(8,128)(2,1)}), bf16[1088,1088]{1,0:T(8,128)(2,1)}) %all-gather.15.cloned.1.call-update) | async-done | bytes 2367504 | tf_op jit(solution)/shard_map/all_gather | solution.py:106
  288.9 164.1 %all-gather.17.cloned.1.call-done = bf16[1088,4352]{1,0:T(8,128)(2,1)} async-done(((bf16[272,4352]{1,0:T(8,128)(2,1)}), bf16[1088,4352]{1,0:T(8,128)(2,1)}) %all-gather.17.cloned.1.call-update) | async-done | bytes 9469968 | tf_op jit(solution)/shard_map/all_gather | solution.py:107
  453.0 17.3 fusion.59
  470.3 158.8 %all-gather.19.cloned.1.call-done = bf16[4352,1088]{1,0:T(8,128)(2,1)} async-done(((bf16[1088,1088]{1,0:T(8,128)(2,1)}), bf16[4352,1088]{1,0:T(8,128)(2,1)}) %all-gather.19.cloned.1.call-update) | async-done | bytes 9469968 | tf_op jit(solution)/shard_map/all_gather | solution.py:108
  673.4 22.1 %while.58 = (s32[]{:T(128)}, f32[256,17,64]{0,2,1:T(8,128)}, s32[1,5]{1,0:T(1,128)S(1)}, bf16[2048,1088]{0,1:T(8,128)(2,1)}, bf16[256,17,64]{0,2,1:T(8,128)(2,1)...) while((s32[]{:T(128)}, f32[256,17,64]{0,2,1:T(8,128)}, ...), condition=%wide.region_23.24_spmd.clone, body=%wide.region_17.23_spmd.clone.sunk | while | flops 869953280 | bytes 29282612 | solution.py:62
  675.2 15.0 conditional.10
  697.0 11.9 all-gather.23.cloned.1.call-done
  710.1 106.8 %while.59 = (s32[]{:T(128)}, f32[256,17,64]{0,2,1:T(8,128)S(1)}, f32[256,17,64]{0,2,1:T(8,128)}, s32[1,5]{1,0:T(1,128)S(1)}, bf16[2048,1088]{0,1:T(8,128)(2,1)},...) while((s32[]{:T(128)}, f32[256,17,64]{0,2,1:T(8,128)S(1)}, ...), condition=%wide.region_30.31_spmd.clone, body=%wide.region_24.30_spmd.clone.sunk | while | flops 1164357120 | bytes 50789280 | solution.py:62
  711.8 25.3 %conditional.11 = ((f32[256,17,64]{0,2,1:T(8,128)S(1)}, f32[256,17,64]{0,2,1:T(8,128)})) conditional(s32[]{:T(128)} %convert_element_type.338, (f32[256,17,64]{0,2,1:T(8,128)S(1)}, f32[256,17,64]{0,2,1:T(8,128)}) %tuple.207, (pred[512,256]{1,0:T(8,128)(4,1)S(1)}, s32[]{:T(128)}, bf16[2048,1088]{0,1:T(8,128)(2,1)}, ...), branch_computations={%region_28.28_spmd, %region_29.29_spmd} | conditional | flops 1163689984 | bytes 50641020 | solution.py:284
  738.8 24.8 %conditional.11 = ((f32[256,17,64]{0,2,1:T(8,128)S(1)}, f32[256,17,64]{0,2,1:T(8,128)})) conditional(s32[]{:T(128)} %convert_element_type.338, (f32[256,17,64]{0,2,1:T(8,128)S(1)}, f32[256,17,64]{0,2,1:T(8,128)}) %tuple.207, (pred[512,256]{1,0:T(8,128)(4,1)S(1)}, s32[]{:T(128)}, bf16[2048,1088]{0,1:T(8,128)(2,1)}, ...), branch_computations={%region_28.28_spmd, %region_29.29_spmd} | conditional | flops 1163689984 | bytes 50641020 | solution.py:284
  765.3 24.8 %conditional.11 = ((f32[256,17,64]{0,2,1:T(8,128)S(1)}, f32[256,17,64]{0,2,1:T(8,128)})) conditional(s32[]{:T(128)} %convert_element_type.338, (f32[256,17,64]{0,2,1:T(8,128)S(1)}, f32[256,17,64]{0,2,1:T(8,128)}) %tuple.207, (pred[512,256]{1,0:T(8,128)(4,1)S(1)}, s32[]{:T(128)}, bf16[2048,1088]{0,1:T(8,128)(2,1)}, ...), branch_computations={%region_28.28_spmd, %region_29.29_spmd} | conditional | flops 1163689984 | bytes 50641020 | solution.py:284
  791.8 24.9 %conditional.11 = ((f32[256,17,64]{0,2,1:T(8,128)S(1)}, f32[256,17,64]{0,2,1:T(8,128)})) conditional(s32[]{:T(128)} %convert_element_type.338, (f32[256,17,64]{0,2,1:T(8,128)S(1)}, f32[256,17,64]{0,2,1:T(8,128)}) %tuple.207, (pred[512,256]{1,0:T(8,128)(4,1)S(1)}, s32[]{:T(128)}, bf16[2048,1088]{0,1:T(8,128)(2,1)}, ...), branch_computations={%region_28.28_spmd, %region_29.29_spmd} | conditional | flops 1163689984 | bytes 50641020 | solution.py:284
  837.8 11.6 fusion.93
  849.7 218.1 %reduce-scatter.5.cloned.1.call-done = f32[272,3264]{1,0:T(8,128)} async-done(((f32[1088,3264]{1,0:T(8,128)}), f32[272,3264]{1,0:T(8,128)}) %reduce-scatter.5.cloned.1.call-update) | async-done | bytes 3551248 | tf_op jit(solution)/shard_map/reduce_scatter | solution.py:66
  1067.9 319.1 %reduce-scatter.9.cloned.1.call-done = f32[272,4352]{1,0:T(8,128)} async-done(((f32[1088,4352]{1,0:T(8,128)}), f32[272,4352]{1,0:T(8,128)}) %reduce-scatter.9.cloned.1.call-update) | async-done | bytes 4734992 | tf_op jit(solution)/shard_map/reduce_scatter | solution.py:66
  1387.0 336.0 %reduce-scatter.11.cloned.1.call-done = f32[1088,1088]{1,0:T(8,128)} async-done(((f32[4352,1088]{1,0:T(8,128)}), f32[1088,1088]{1,0:T(8,128)}) %reduce-scatter.11.cloned.1.call-update) | async-done | bytes 4734992 | tf_op jit(solution)/shard_map/reduce_scatter | solution.py:66
  1741.4 20.6 %all-reduce.20 = (f32[1088]{0:T(1024)S(1)}, f32[1088]{0:T(1024)S(1)}, f32[1088]{0:T(1024)S(1)}, f32[1088]{0:T(1024)S(1)}, f32[1088]{0:T(1024)S(1)}, /*index=5*/f...) all-reduce(f32[1088]{0:T(1024)S(1)} %get-tuple-element.1213, ...), channel_id=2, replica_groups=mesh['ctx'=8,'wsh'=4] {'wsh'}, use_global_device_ids=true, to_apply=%region_34.35.clone | all-reduce | flops 13056 | bytes 104448
  1762.6 24.8 %all-reduce.18 = (f32[272]{0:T(512)}, f32[272]{0:T(512)}, f32[272]{0:T(512)}, f32[272]{0:T(512)}, f32[272]{0:T(512)}, /*index=5*/f32[272]{0:T(512)}, f32[272]{0:T(512)}, f32[1088]{0:T(1024)}, f32[272]{0:T(512)}) all-reduce(f32[272]{0:T(512)S(1)} %dynamic-slice.10, ...), channel_id=1, replica_groups=mesh['ctx'=8,'wsh'=4] {'ctx'}, use_global_device_ids=true, to_apply=%region_35.36 | all-reduce | flops 3264 | bytes 26112 | tf_op jit(solution)/shard_map/psum | solution.py:67
  1790.1 133.4 %all-reduce.24.cloned.1.call-done = (f32[272,3264]{1,0:T(8,128)}, f32[272,1088]{1,0:T(8,128)}, f32[272,4352]{1,0:T(8,128)}, f32[1088,1088]{1,0:T(8,128)}) async-done(((f32[272,3264]{1,0:T(8,128)}, f32[272,1088]{1,0:T(8,128)}, f32[272,4352]{1,0:T(8,128)}, f32[1088,1088]{1,0:T(8,128)}), (f32[272,3264]{1,0:T(8,128)}, f32[272,1088]{1,0:T(8,128)}, f32[272,4352]{1,0:T(8,128)}, ...) | async-done | bytes 14204944 | tf_op jit(solution)/shard_map/psum | solution.py:67
  (306 shorter events, 273.7 us)
Async XLA Ops:
  7.2 41.9 %copy-start.6 = (bf16[1,256,1088]{1,2,0:T(8,128)(2,1)S(1)}, bf16[1,256,1088]{1,2,0:T(8,128)(2,1)}, u32[]{:S(2)}) copy-start(bf16[1,256,1088]{1,2,0:T(8,128)(2,1)} %param.28) | copy-start | bytes 1671172
  7.2 137.4 %all-gather.9.cloned.1.call-start = ((), (), s32[]{:S(2)}) async-start(), calls=%async_computation.4 | async-start | bytes 9052160 | tf_op jit(solution)/shard_map/all_gather | solution.py:105
  7.9 182.9 %all-gather.11.cloned.1.call-start = ((), (), s32[]{:S(2)}) async-start(), calls=%async_computation.5 | async-start | bytes 5013504 | tf_op jit(solution)/shard_map/all_gather | solution.py:178
  47.8 103.5 %copy-start.18 = (f32[1088]{0:T(1024)}, f32[1088]{0:T(1024)S(1)}, u32[]{:S(2)}) copy-start(f32[1088]{0:T(1024)S(1)} %convert_element_type.191) | copy-start | bytes 13060
  47.8 103.5 %copy-start.16 = (f32[1088]{0:T(1024)}, f32[1088]{0:T(1024)S(1)}, u32[]{:S(2)}) copy-start(f32[1088]{0:T(1024)S(1)} %convert_element_type.190) | copy-start | bytes 13060
  49.1 102.2 %copy-start.22 = (f32[256]{0:T(256)}, f32[256]{0:T(256)S(1)}, u32[]{:S(2)}) copy-start(f32[256]{0:T(256)S(1)} %broadcast_multiply_fusion.5) | copy-start | bytes 3076
  49.3 102.0 %copy-start.26 = (f32[256]{0:T(256)}, f32[256]{0:T(256)S(1)}, u32[]{:S(2)}) copy-start(f32[256]{0:T(256)S(1)} %add_rsqrt_fusion.1) | copy-start | bytes 3076
  153.9 77.3 %all-gather.13.cloned.1.call-start = ((), (), s32[]{:S(2)}) async-start(), calls=%async_computation.6 | async-start | bytes 5013504 | tf_op jit(solution)/shard_map/all_gather | solution.py:179
  157.0 128.6 %all-gather.15.cloned.1.call-start = ((), (), s32[]{:S(2)}) async-start(), calls=%async_computation.7 | async-start | bytes 3133440 | tf_op jit(solution)/shard_map/all_gather | solution.py:106
  157.6 295.4 %all-gather.17.cloned.1.call-start = ((), (), s32[]{:S(2)}) async-start(), calls=%async_computation.8 | async-start | bytes 11837440 | tf_op jit(solution)/shard_map/all_gather | solution.py:107
  158.2 73.2 %copy-start = (bf16[256,1088]{0,1:T(8,128)(2,1)S(1)}, bf16[256,1088]{0,1:T(8,128)(2,1)}, u32[]{:S(2)}) copy-start(bf16[256,1088]{0,1:T(8,128)(2,1)} %get-tuple-element.1331) | copy-start | bytes 1671172
  158.2 470.9 %all-gather.19.cloned.1.call-start = ((), (), s32[]{:S(2)}) async-start(), calls=%async_computation.9 | async-start | bytes 12533760 | tf_op jit(solution)/shard_map/all_gather | solution.py:108
  158.7 538.2 %all-gather.21.cloned.1.call-start = ((), (), s32[]{:S(2)}) async-start(), calls=%async_computation.10 | async-start | bytes 5013504 | tf_op jit(solution)/shard_map/all_gather | solution.py:289
  159.0 294.0 %copy-start.20 = (f32[1088]{0:T(1024)}, f32[1088]{0:T(1024)S(1)}, u32[]{:S(2)}) copy-start(f32[1088]{0:T(1024)S(1)} %convert_element_type.201) | copy-start | bytes 13060
  159.5 549.4 %all-gather.23.cloned.1.call-start = ((), (), s32[]{:S(2)}) async-start(), calls=%async_computation.11 | async-start | bytes 5013504 | tf_op jit(solution)/shard_map/all_gather | solution.py:290
  288.7 352.2 %copy-start.2 = (f32[256,1088]{0,1:T(8,128)}, f32[256,1088]{0,1:T(8,128)S(1)}, u32[]{:S(2)}) copy-start(f32[256,1088]{0,1:T(8,128)S(1)} %get-tuple-element.1336) | copy-start | bytes 3342340
  288.9 340.1 %copy-start.14 = (bf16[1,256,1088]{1,2,0:T(8,128)(2,1)S(1)}, bf16[1,256,1088]{1,2,0:T(8,128)(2,1)}, u32[]{:S(2)}) copy-start(bf16[1,256,1088]{1,2,0:T(8,128)(2,1)} %param.30) | copy-start | bytes 1671172
  645.0 204.7 %reduce-scatter.7.cloned.1.call-start = ((), (), s32[]{:S(2)}) async-start(), calls=%async_computation.13 | async-start | bytes 6266880 | tf_op jit(solution)/shard_map/reduce_scatter | solution.py:66
  649.7 418.1 %reduce-scatter.5.cloned.1.call-start = ((), (), s32[]{:S(2)}) async-start(), calls=%async_computation.12 | async-start | bytes 18104320 | tf_op jit(solution)/shard_map/reduce_scatter | solution.py:66
  695.5 14.6 copy-start.1
  826.0 561.0 %reduce-scatter.9.cloned.1.call-start = ((), (), s32[]{:S(2)}) async-start(), calls=%async_computation.14 | async-start | bytes 23674880 | tf_op jit(solution)/shard_map/reduce_scatter | solution.py:66
  837.7 885.3 %reduce-scatter.11.cloned.1.call-start = ((), (), s32[]{:S(2)}) async-start(), calls=%async_computation.15 | async-start | bytes 25067520 | tf_op jit(solution)/shard_map/reduce_scatter | solution.py:66
  849.4 1074.1 %all-reduce.24.cloned.1.call-start = ((), (), s32[]{:S(2)}) async-start(), calls=%async_computation.16 | async-start | bytes 29245440 | tf_op jit(solution)/shard_map/psum | solution.py:67
  1734.9 52.5 %copy-start.5 = (f32[256,1088]{0,1:T(8,128)S(1)}, f32[256,1088]{0,1:T(8,128)}, u32[]{:S(2)}) copy-start(f32[256,1088]{0,1:T(8,128)} %copy-done.4) | copy-start | bytes 3342340
  (32 other events, 112.8 us)
Sparse Core Ops, SparseCore 0:
  9.6 134.9 all-gather.8
  154.0 36.7 all-gather.10
  192.7 38.4 all-gather.12
  232.7 52.8 all-gather.14
  287.0 165.9 all-gather.16
  454.4 174.5 all-gather.18
  630.9 37.4 all-gather.20
  670.3 38.5 all-gather.22
  711.8 90.0 reduce-scatter.6
  826.1 241.7 reduce-scatter.4
  1070.3 316.6 reduce-scatter.8
  1389.2 333.7 reduce-scatter.10
  1727.0 196.4 all-reduce.23
where the time goes:
time: 1950 us; the launch traced here: 1940 us
  waiting for transfers between devices  1550 us (79%)
  matrix products  190 us (10%)
  blocking collectives  96 us (5%)
  local copies, waits for them, and re-layouts  49.6 us (3%)
  other arithmetic  29.6 us (2%)
    reduce_scatter x4, waiting for transfers between devices, sectioned_sum(): shares = lax.psum_scatter(partials, 'wsh', scatter_dimension=0, tiled=True)  873 us
    all_gather x1, waiting for transfers between devices, on_device(): lax.all_gather(shards[2], 'wsh', axis=0, tiled=True)  164 us
    all_gather x1, waiting for transfers between devices, on_device(): lax.all_gather(shards[3], 'wsh', axis=0, tiled=True)  159 us
    psum x1, waiting for transfers between devices, sectioned_sum(): return lax.psum(shares, 'ctx')  133 us
    all_gather x1, waiting for transfers between devices, on_device(): lax.all_gather(shards[0], 'wsh', axis=0, tiled=True)  95.3 us
    unnamed x2, blocking collectives  49.9 us
    all_gather x1, waiting for transfers between devices, on_device(): lax.all_gather(value_rows, 'ctx', axis=0, tiled=True)  40.4 us
  transfers between devices with their start and end apart: 13, of which 11 were waited for; matrix products, arithmetic and copies ran while one was open for 12% of the time, Pallas kernels for 0%

commit v1 on v0

--- a/solution.py
+++ b/solution.py
@@ -1,8 +1,11 @@
+import functools
 import math
 
 import jax
 import jax.numpy as jnp
 from jax import lax
+from jax.experimental import pallas as pl
+from jax.experimental.pallas import tpu as pltpu
 from jax.sharding import PartitionSpec as P
 
 D = 1088
@@ -339,6 +342,866 @@
     )
 
 
+SLOTS = 5
+WIDE = 384
+ROWS = 256
+CHIPS = 4
+MESH_ID = pl.DeviceIdType.MESH
+F32, BF16 = (jnp.float32, jnp.bfloat16)
+NEG = -1e30
+HEAD_TABLE = ((0, 5, 9, 13, -40), (1, 6, 10, 14, -40), (2, 7, 11, 15, -40), (3, 4, 8, 12, 16))
+
+
+def nn(left, right):
+    return jnp.dot(left, right, preferred_element_type=F32)
+
+
+def position():
+    c, z = (lax.axis_index("ctx"), lax.axis_index("wsh"))
+    return c // 2, c % 2, z
+
+
+def greet(t, p, z):
+    barrier = pltpu.get_barrier_semaphore()
+    for k in range(1, CHIPS):
+        pl.semaphore_signal(
+            barrier, inc=1, device_id=((t + k) % CHIPS * 2 + p, z), device_id_type=MESH_ID
+        )
+    pl.semaphore_signal(barrier, inc=1, device_id=(t * 2 + 1 - p, z), device_id_type=MESH_ID)
+    pl.semaphore_wait(barrier, CHIPS)
+
+
+def to_chip(src, dst, send, recv, t, p, z, k):
+    return pltpu.make_async_remote_copy(
+        src_ref=src,
+        dst_ref=dst,
+        send_sem=send,
+        recv_sem=recv,
+        device_id=((t + k) % CHIPS * 2 + p, z),
+        device_id_type=MESH_ID,
+    )
+
+
+def to_twin(src, dst, send, recv, t, p, z):
+    return pltpu.make_async_remote_copy(
+        src_ref=src,
+        dst_ref=dst,
+        send_sem=send,
+        recv_sem=recv,
+        device_id=(t * 2 + 1 - p, z),
+        device_id_type=MESH_ID,
+    )
+
+
+def rows16(start, size):
+    return pl.ds(pl.multiple_of(start, 16), size)
+
+
+def weight_copies(half, whole, block, keep, step, local, send, recv, t, p, z, base=0):
+    copies = []
+    for i in range(4):
+        copies.append(
+            pltpu.make_async_copy(
+                half.at[i, rows16(base, keep)],
+                whole.at[rows16(i * block + p * step, keep)],
+                local.at[i],
+            )
+        )
+        copies.append(
+            to_twin(
+                half.at[i, rows16(base + p * (keep - step), step)],
+                whole.at[rows16(i * block + p * keep, step)],
+                send.at[i],
+                recv.at[i],
+                t,
+                p,
+                z,
+            )
+        )
+    return copies
+
+
+def params(number, mib=56):
+    return pltpu.CompilerParams(
+        collective_id=number, has_side_effects=True, vmem_limit_bytes=mib * 2**20
+    )
+
+
+def vmem(count):
+    return [pl.BlockSpec(memory_space=pltpu.VMEM)] * count
+
+
+def project_kernel(
+    x, half, gain, shift, bias_q, bias_v,
+    q_out, k_out, v_out, h_out, whole,
+    send, recv, w_local, w_send, w_recv, kv_send, kv_recv,
+):
+    t, p, z = position()
+    greet(t, p, z)
+    weights = weight_copies(half, whole, 272, 144, 128, w_local, w_send, w_recv, t, p, z)
+    for copy in weights:
+        copy.start()
+    normed, _ = normalize(x[...].astype(F32))
+    h_out[t] = (normed * gain[...] + shift[...]).astype(BF16)
+    sends = [
+        to_chip(h_out.at[t], h_out.at[t], send.at[k], recv.at[k], t, p, z, k)
+        for k in range(1, CHIPS)
+    ]
+    for copy in sends:
+        copy.start()
+    for copy in weights:
+        copy.wait()
+
+    def block(k, carry):
+        src = (t + CHIPS - k) % CHIPS
+
+        @pl.when(k > 0)
+        def _():
+            to_chip(h_out.at[src], h_out.at[src], send.at[k], recv.at[k], t, p, z, 0 * k + 1).wait_recv()
+
+        h = h_out[src]
+        q_out[src] = ((nn(h, whole[:, :WIDE]) + bias_q[...]).astype(BF16) * 0.125).astype(BF16)
+        mine = src * 2 + p
+        k_out[mine] = nn(h, whole[:, WIDE : 2 * WIDE]).astype(BF16)
+        to_twin(k_out.at[mine], k_out.at[mine], kv_send.at[k], kv_recv.at[k], t, p, z).start()
+        v_out[mine] = (nn(h, whole[:, 2 * WIDE :]) + bias_v[...]).astype(BF16)
+        to_twin(
+            v_out.at[mine], v_out.at[mine], kv_send.at[k + CHIPS], kv_recv.at[k + CHIPS], t, p, z
+        ).start()
+        return carry
+
+    lax.fori_loop(0, CHIPS, block, 0)
+    for copy in sends:
+        copy.wait_send()
+    for k in range(CHIPS):
+        other = (t + CHIPS - k) % CHIPS * 2 + 1 - p
+        mine = (t + CHIPS - k) % CHIPS * 2 + p
+        for ref, j in ((k_out, k), (v_out, k + CHIPS)):
+            to_twin(ref.at[mine], ref.at[mine], kv_send.at[j], kv_recv.at[j], t, p, z).wait_send()
+            to_twin(ref.at[other], ref.at[other], kv_send.at[j], kv_recv.at[j], t, p, z).wait_recv()
+
+
+def project(x, half, gain, shift, bias_q, bias_v):
+    blocks = jax.ShapeDtypeStruct((CHIPS, ROWS, WIDE), BF16)
+    keys = jax.ShapeDtypeStruct((2 * CHIPS, ROWS, WIDE), BF16)
+    dma = pltpu.SemaphoreType.DMA
+    return pl.pallas_call(
+        project_kernel,
+        out_shape=(
+            blocks, keys, keys,
+            jax.ShapeDtypeStruct((CHIPS, ROWS, D), BF16),
+            jax.ShapeDtypeStruct((D, 3 * WIDE), BF16),
+        ),
+        in_specs=vmem(6),
+        out_specs=tuple(vmem(5)),
+        scratch_shapes=[
+            dma((CHIPS,)), dma((CHIPS,)), dma((4,)), dma((4,)), dma((4,)),
+            dma((2 * CHIPS,)), dma((2 * CHIPS,)),
+        ],
+        compiler_params=params(1),
+        name="project",
+    )(x, half, gain, shift, bias_q, bias_v)
+
+
+def tile_bounds(lengths, block):
+    ends = [lengths[0]]
+    for i in range(1, 4):
+        ends.append(ends[-1] + lengths[i])
+    first = block * ROWS
+    start_first = 0 * first
+    for end in ends:
+        start_first = jnp.where(first >= end, end, start_first)
+    free = jnp.minimum(block, ends[0] // ROWS)
+    resume = jnp.maximum(free + 1, start_first // ROWS)
+    masked = jnp.where(free < block, 1 + jnp.maximum(block - resume, 0), 0)
+    query_pos = first + lax.broadcasted_iota(jnp.int32, (1, ROWS), 1)
+    start = jnp.zeros((1, ROWS), jnp.int32)
+    for end in ends:
+        start = jnp.where(query_pos >= end, end, start)
+    return ends[0], query_pos, start, free, resume, masked
+
+
+def visible(key_block, prompt, query_pos, start):
+    key_pos = key_block * ROWS + lax.broadcasted_iota(jnp.int32, (ROWS, ROWS), 0)
+    return (key_pos <= query_pos) & ((key_pos < prompt) | (key_pos >= start))
+
+
+def half_of(rows, h):
+    lane = lax.broadcasted_iota(jnp.int32, rows.shape, 1)
+    return jnp.where((lane >= h * HEAD_DIM) & (lane < (h + 1) * HEAD_DIM), rows, jnp.zeros_like(rows))
+
+
+def attend_kernel(lengths, parity, q, k, v, mixed, lse, turned):
+    slab = pl.program_id(0)
+    for j in range(2 * CHIPS):
+        turned[j] = v[j].astype(F32).T.astype(BF16)
+
+    def run(heads):
+        def one(i, carry):
+            block = 2 * i + parity[0]
+            prompt, query_pos, start, free, resume, masked = tile_bounds(lengths, block)
+            queries = [half_of(q[i], h) for h in heads]
+
+            def tile(j, state, mask):
+                keys = k[j]
+                values = turned[j]
+                new = []
+                for h, (peak, total, accum) in zip(heads, state):
+                    scores = cols_product(keys, queries[h])
+                    if mask is not None:
+                        scores = jnp.where(mask, scores, NEG)
+                    peak_new = jnp.maximum(peak, jnp.max(scores, 0, keepdims=True))
+                    factor = jnp.exp(peak - peak_new)
+                    expos = jnp.exp(scores - peak_new)
+                    total_new = total * factor + jnp.sum(expos, 0, keepdims=True)
+                    part = values[h * HEAD_DIM : (h + 1) * HEAD_DIM]
+                    accum_new = accum * factor + nn(part, expos.astype(BF16))
+                    new.append((peak_new, total_new, accum_new))
+                return tuple(new)
+
+            state = tuple(
+                (
+                    jnp.full((1, ROWS), NEG, F32),
+                    jnp.zeros((1, ROWS), F32),
+                    jnp.zeros((HEAD_DIM, ROWS), F32),
+                )
+                for _ in heads
+            )
+            state = tile(block, state, visible(block, prompt, query_pos, start))
+            state = lax.fori_loop(0, free, lambda j, s: tile(j, s, None), state)
+
+            def other(m, s):
+                j = jnp.where(m == 0, free, resume + m - 1)
+                return tile(j, s, visible(j, prompt, query_pos, start))
+
+            state = lax.fori_loop(0, masked, other, state)
+            outs = []
+            for h, (peak, total, accum) in zip(heads, state):
+                outs.append(accum / total)
+                lse[0, pl.ds(h * CHIPS + i, 1), :] = peak + jnp.log(total)
+            if len(heads) == 1:
+                outs.append(jnp.zeros((HEAD_DIM, ROWS), F32))
+            mixed[i] = jnp.concatenate(outs, 0).T.astype(BF16)
+            return carry
+
+        lax.fori_loop(0, CHIPS, one, 0)
+
+    @pl.when(slab < SLOTS // 2)
+    def _():
+        run((0, 1))
+
+    @pl.when(slab >= SLOTS // 2)
+    def _():
+        lse[...] = jnp.zeros_like(lse)
+        run((0,))
+
+
+def slab_spec(count):
+    return pl.BlockSpec((count, ROWS, 128), lambda s, *_: (0, 0, s))
+
+
+def attend(lengths, parity, q, k, v):
+    return pl.pallas_call(
+        attend_kernel,
+        out_shape=(
+            jax.ShapeDtypeStruct((CHIPS, ROWS, WIDE), BF16),
+            jax.ShapeDtypeStruct((3, 2 * CHIPS, ROWS), F32),
+        ),
+        grid_spec=pltpu.PrefetchScalarGridSpec(
+            num_scalar_prefetch=2,
+            grid=(3,),
+            in_specs=[slab_spec(CHIPS), slab_spec(2 * CHIPS), slab_spec(2 * CHIPS)],
+            out_specs=(
+                slab_spec(CHIPS),
+                pl.BlockSpec((1, 2 * CHIPS, ROWS), lambda s, *_: (s, 0, 0)),
+            ),
+            scratch_shapes=[pltpu.VMEM((2 * CHIPS, 128, ROWS), BF16)],
+        ),
+        compiler_params=pltpu.CompilerParams(vmem_limit_bytes=48 * 2**20),
+        cost_estimate=pl.CostEstimate(flops=4 * 10**9, bytes_accessed=5 * 10**6, transcendentals=6 * 10**6),
+        name="attend",
+    )(lengths, parity, q, k, v)
+
+
+def attend_back_kernel(
+    lengths, parity, q, k, v, mixed, grad, lse, dq, dk, dv, turned, acc_k, acc_v
+):
+    slab = pl.program_id(0)
+    for j in range(2 * CHIPS):
+        turned[j] = k[j].astype(F32).T.astype(BF16)
+    acc_k[...] = jnp.zeros_like(acc_k)
+    acc_v[...] = jnp.zeros_like(acc_v)
+
+    def run(heads):
+        def one(i, carry):
+            block = 2 * i + parity[0]
+            prompt, query_pos, start, free, resume, masked = tile_bounds(lengths, block)
+            queries = [half_of(q[i], h) for h in heads]
+            grads = [half_of(grad[i], h) for h in heads]
+            product = (grad[i].astype(F32) * mixed[i].astype(F32)).T
+            deltas = [
+                jnp.sum(product[h * HEAD_DIM : (h + 1) * HEAD_DIM], 0, keepdims=True) for h in heads
+            ]
+            sums = [lse[0, pl.ds(h * CHIPS + i, 1), :] for h in heads]
+
+            def tile(j, state, mask):
+                keys, values, keys_t = (k[j], v[j], turned[j])
+                new = []
+                add_k, add_v = (None, None)
+                for h, accum in zip(heads, state):
+                    scores = cols_product(keys, queries[h]) - sums[h]
+                    if mask is not None:
+                        scores = jnp.where(mask, scores, NEG)
+                    probs = jnp.exp(scores)
+                    grad_probs = cols_product(values, grads[h])
+                    ds = (probs * (grad_probs - deltas[h])).astype(BF16)
+                    part_v = nn(probs.astype(BF16), grads[h])
+                    part_k = nn(ds, queries[h])
+                    add_v = part_v if add_v is None else add_v + part_v
+                    add_k = part_k if add_k is None else add_k + part_k
+                    new.append(accum + nn(keys_t[h * HEAD_DIM : (h + 1) * HEAD_DIM], ds))
+                acc_v[j] += add_v
+                acc_k[j] += add_k
+                return tuple(new)
+
+            state = tuple(jnp.zeros((HEAD_DIM, ROWS), F32) for _ in heads)
+            state = tile(block, state, visible(block, prompt, query_pos, start))
+            state = lax.fori_loop(0, free, lambda j, s: tile(j, s, None), state)
+
+            def other(m, s):
+                j = jnp.where(m == 0, free, resume + m - 1)
+                return tile(j, s, visible(j, prompt, query_pos, start))
+
+            state = list(lax.fori_loop(0, masked, other, state))
+            if len(heads) == 1:
+                state.append(jnp.zeros((HEAD_DIM, ROWS), F32))
+            dq[i] = (jnp.concatenate(state, 0) * 0.125).T.astype(BF16)
+            return carry
+
+        lax.fori_loop(0, CHIPS, one, 0)
+
+    @pl.when(slab < SLOTS // 2)
+    def _():
+        run((0, 1))
+
+    @pl.when(slab >= SLOTS // 2)
+    def _():
+        run((0,))
+
+    dk[...] = acc_k[...].astype(BF16)
+    dv[...] = acc_v[...].astype(BF16)
+
+
+def attend_back(lengths, parity, q, k, v, mixed, grad, lse):
+    few, many = (slab_spec(CHIPS), slab_spec(2 * CHIPS))
+    return pl.pallas_call(
+        attend_back_kernel,
+        out_shape=(
+            jax.ShapeDtypeStruct((CHIPS, ROWS, WIDE), BF16),
+            jax.ShapeDtypeStruct((2 * CHIPS, ROWS, WIDE), BF16),
+            jax.ShapeDtypeStruct((2 * CHIPS, ROWS, WIDE), BF16),
+        ),
+        grid_spec=pltpu.PrefetchScalarGridSpec(
+            num_scalar_prefetch=2,
+            grid=(3,),
+            in_specs=[
+                few, many, many, few, few,
+                pl.BlockSpec((1, 2 * CHIPS, ROWS), lambda s, *_: (s, 0, 0)),
+            ],
+            out_specs=(few, many, many),
+            scratch_shapes=[
+                pltpu.VMEM((2 * CHIPS, 128, ROWS), BF16),
+                pltpu.VMEM((2 * CHIPS, ROWS, 128), F32),
+                pltpu.VMEM((2 * CHIPS, ROWS, 128), F32),
+            ],
+        ),
+        compiler_params=pltpu.CompilerParams(vmem_limit_bytes=48 * 2**20),
+        cost_estimate=pl.CostEstimate(flops=10 * 10**9, bytes_accessed=9 * 10**6, transcendentals=6 * 10**6),
+        name="attend_back",
+    )(lengths, parity, q, k, v, mixed, grad, lse)
+
+
+def out_kernel(
+    x, mixed, half, bias, middle, whole, raw, parts, landed, send, recv, w_local, w_send, w_recv
+):
+    t, p, z = position()
+    greet(t, p, z)
+    weights = weight_copies(half, raw, 80, 48, 32, w_local, w_send, w_recv, t, p, z)
+    for copy in weights:
+        copy.start()
+    for copy in weights:
+        copy.wait()
+
+    @pl.when(t == CHIPS - 1)
+    def _():
+        whole[: SLOTS * HEAD_DIM] = raw[...]
+
+    @pl.when(t < CHIPS - 1)
+    def _():
+        for i in range(4):
+            whole[i * HEAD_DIM : (i + 1) * HEAD_DIM] = raw[i * 80 : i * 80 + HEAD_DIM]
+        whole[4 * HEAD_DIM : 5 * HEAD_DIM] = jnp.zeros((HEAD_DIM, D), BF16)
+
+    whole[SLOTS * HEAD_DIM :] = jnp.zeros((WIDE - SLOTS * HEAD_DIM, D), BF16)
+
+    def part(k, carry):
+        parts[k] = nn(mixed[(t + k) % CHIPS], whole[...]).astype(BF16)
+        to_chip(parts.at[k], landed.at[k], send.at[k], recv.at[k], t, p, z, k).start()
+        return carry
+
+    lax.fori_loop(1, CHIPS, part, 0)
+    total = x[...].astype(F32) + bias[...] + nn(mixed[t], whole[...])
+    for k in range(1, CHIPS):
+        to_chip(parts.at[k], landed.at[k], send.at[k], recv.at[k], t, p, z, k).wait()
+        total = total + landed[k].astype(F32)
+    middle[...] = total
+
+
+def out_project(x, mixed, half, bias):
+    dma = pltpu.SemaphoreType.DMA
+    return pl.pallas_call(
+        out_kernel,
+        out_shape=(
+            jax.ShapeDtypeStruct((ROWS, D), F32),
+            jax.ShapeDtypeStruct((WIDE, D), BF16),
+        ),
+        in_specs=vmem(4),
+        out_specs=tuple(vmem(2)),
+        scratch_shapes=[
+            pltpu.VMEM((SLOTS * HEAD_DIM, D), BF16),
+            pltpu.VMEM((CHIPS, ROWS, D), BF16),
+            pltpu.VMEM((CHIPS, ROWS, D), BF16),
+            dma((CHIPS,)), dma((CHIPS,)), dma((4,)), dma((4,)), dma((4,)),
+        ],
+        compiler_params=params(2),
+        name="out_project",
+    )(x, mixed, half, bias)
+
+
+def feed_kernel(
+    middle, cot, halves, up_bias, gain, shift, down_bias, out_w, mixed,
+    output, grad_mid, gh_heads, g_out, g_feed, sums, up_sum,
+    up, down, hid, cots, act, gpre, part_o, part_h, land_o, land_h, gmid, full_up, full_down, land_up, land_down, raw, land_out,
+    send, recv, w_local, w_send, w_recv, g_send, g_recv,
+):
+    t, p, z = position()
+    greet(t, p, z)
+    weights = weight_copies(
+        halves, up, 272, 144, 128, w_local.at[0], w_send.at[0], w_recv.at[0], t, p, z
+    ) + weight_copies(
+        halves, down, 272, 144, 128, w_local.at[1], w_send.at[1], w_recv.at[1], t, p, z, 144
+    )
+    normed, inverse = normalize(middle[...])
+    hid[t] = (normed * gain[...] + shift[...]).astype(BF16)
+    cots[t] = cot[...]
+    for k in range(1, CHIPS):
+        to_chip(hid.at[t], hid.at[t], send.at[0, k], recv.at[0, k], t, p, z, k).start()
+    for copy in weights:
+        copy.start()
+    for k in range(1, CHIPS):
+        to_chip(cots.at[t], cots.at[t], send.at[1, k], recv.at[1, k], t, p, z, k).start()
+    for copy in weights:
+        copy.wait()
+    up_sum[...] = jnp.zeros_like(up_sum)
+
+    def block(k, carry):
+        src = (t + CHIPS - k) % CHIPS
+
+        @pl.when(k > 0)
+        def _():
+            to_chip(hid.at[src], hid.at[src], send.at[0, k], recv.at[0, k], t, p, z, 1).wait_recv()
+
+        pre = nn(hid[src], up[...]) + up_bias[...]
+        cdf = 0.5 * (1.0 + lax.erf(pre * math.sqrt(0.5)))
+        slope = cdf + pre * (jnp.exp(-0.5 * pre * pre) * (1.0 / math.sqrt(2.0 * math.pi)))
+        act[src] = (pre * cdf).astype(BF16)
+
+        @pl.when(k > 0)
+        def _():
+            to_chip(cots.at[src], cots.at[src], send.at[1, k], recv.at[1, k], t, p, z, 1).wait_recv()
+
+        grad = cols_product(cots[src], down[...]) * slope
+        low = grad.astype(BF16)
+        gpre[src] = low
+        up_sum[...] += jnp.sum(low.astype(F32), 0, keepdims=True)
+        part_h[src] = cols_product(low, up[...]).astype(BF16)
+
+        @pl.when(k > 0)
+        def _():
+            to_chip(part_h.at[src], land_h.at[t], send.at[2, k], recv.at[2, k], t, p, z, CHIPS - k).start()
+
+        part_o[src] = nn(act[src], down[...]).astype(BF16)
+        return carry
+
+    lax.fori_loop(0, CHIPS, block, 0)
+
+    for k in range(1, CHIPS):
+        src = (t + CHIPS - k) % CHIPS
+        to_chip(part_o.at[src], land_o.at[t], send.at[3, k], recv.at[3, k], t, p, z, CHIPS - k).start()
+
+    def stack(ref):
+        return ref[...].reshape(CHIPS * ROWS, ref.shape[-1])
+
+    full_up[...] = rows_product(stack(hid), stack(gpre)).astype(BF16)
+    full_down[...] = rows_product(stack(act), stack(cots)).astype(BF16)
+    swaps = []
+    for i in range(4):
+        for j, (full, land) in enumerate(((full_up, land_up), (full_down, land_down))):
+            swaps.append(
+                to_twin(
+                    full.at[rows16(i * 272 + (1 - p) * 128, 144)],
+                    land.at[i],
+                    g_send.at[j, i],
+                    g_recv.at[j, i],
+                    t,
+                    p,
+                    z,
+                )
+            )
+    for copy in swaps:
+        copy.start()
+
+    total = part_h[t].astype(F32)
+    for k in range(1, CHIPS):
+        to_chip(part_h.at[t], land_h.at[t], send.at[2, k], recv.at[2, k], t, p, z, k).wait()
+        total = total + land_h[(t + k) % CHIPS].astype(F32)
+    top = cot[...].astype(F32)
+    grad_middle = top + norm_back(total, normed, inverse, gain[...])
+    grad_mid[...] = grad_middle
+    low = grad_middle.astype(BF16)
+    gmid[t] = low
+    for k in range(1, CHIPS):
+        to_chip(gmid.at[t], gmid.at[t], send.at[4, k], recv.at[4, k], t, p, z, k).start()
+    sums[0:1] = jnp.sum(low.astype(F32), 0, keepdims=True)
+    sums[1:2] = jnp.sum(top, 0, keepdims=True)
+    sums[2:3] = jnp.sum(total * normed, 0, keepdims=True)
+    sums[3:4] = jnp.sum(total, 0, keepdims=True)
+    sums[4:8] = jnp.zeros((4, D), F32)
+
+    for copy in swaps:
+        copy.wait()
+    for i in range(4):
+        for j, (full, land) in enumerate(((full_up, land_up), (full_down, land_down))):
+            own = full[rows16(i * 272 + p * 128, 144)].astype(F32)
+            g_feed[i, j * 144 : (j + 1) * 144] = (own + land[i].astype(F32)).astype(BF16)
+
+    def heads(k, carry):
+        src = (t + CHIPS - k) % CHIPS
+
+        @pl.when(k > 0)
+        def _():
+            to_chip(gmid.at[src], gmid.at[src], send.at[4, k], recv.at[4, k], t, p, z, 1).wait_recv()
+
+        gh_heads[src] = cols_product(gmid[src], out_w[...]).astype(BF16)
+        return carry
+
+    lax.fori_loop(0, CHIPS, heads, 0)
+    grad_out = rows_product(stack(mixed), stack(gmid)).astype(BF16)
+
+    @pl.when(t == CHIPS - 1)
+    def _():
+        raw[...] = grad_out[: SLOTS * HEAD_DIM]
+
+    @pl.when(t < CHIPS - 1)
+    def _():
+        for i in range(4):
+            raw[i * 80 : i * 80 + HEAD_DIM] = grad_out[i * HEAD_DIM : (i + 1) * HEAD_DIM]
+            raw[i * 80 + HEAD_DIM : (i + 1) * 80] = jnp.zeros((16, D), BF16)
+
+    swaps = [
+        to_twin(
+            raw.at[rows16(i * 80 + (1 - p) * 32, 48)],
+            land_out.at[i],
+            g_send.at[2, i],
+            g_recv.at[2, i],
+            t,
+            p,
+            z,
+        )
+        for i in range(4)
+    ]
+    for copy in swaps:
+        copy.start()
+    for copy in swaps:
+        copy.wait()
+    for i in range(4):
+        own = raw[rows16(i * 80 + p * 32, 48)].astype(F32)
+        g_out[i] = (own + land_out[i].astype(F32)).astype(BF16)
+
+    result = middle[...] + down_bias[...] + part_o[t].astype(F32)
+    for k in range(1, CHIPS):
+        to_chip(part_o.at[t], land_o.at[t], send.at[3, k], recv.at[3, k], t, p, z, k).wait()
+        result = result + land_o[(t + k) % CHIPS].astype(F32)
+    output[...] = result.astype(BF16)
+    for k in range(1, CHIPS):
+        to_chip(hid.at[t], hid.at[t], send.at[0, k], recv.at[0, k], t, p, z, k).wait_send()
+        to_chip(cots.at[t], cots.at[t], send.at[1, k], recv.at[1, k], t, p, z, k).wait_send()
+        to_chip(gmid.at[t], gmid.at[t], send.at[4, k], recv.at[4, k], t, p, z, k).wait_send()
+
+
+def feed(middle, cot, halves, up_bias, gain, shift, down_bias, out_w, mixed):
+    dma = pltpu.SemaphoreType.DMA
+    blocks = pltpu.VMEM((CHIPS, ROWS, D), BF16)
+    matrix = pltpu.VMEM((D, D), BF16)
+    piece = pltpu.VMEM((4, 144, D), BF16)
+    return pl.pallas_call(
+        feed_kernel,
+        out_shape=(
+            jax.ShapeDtypeStruct((ROWS, D), BF16),
+            jax.ShapeDtypeStruct((ROWS, D), F32),
+            jax.ShapeDtypeStruct((CHIPS, ROWS, WIDE), BF16),
+            jax.ShapeDtypeStruct((4, 48, D), BF16),
+            jax.ShapeDtypeStruct((4, 288, D), BF16),
+            jax.ShapeDtypeStruct((8, D), F32),
+            jax.ShapeDtypeStruct((1, D), F32),
+        ),
+        in_specs=vmem(9),
+        out_specs=tuple(vmem(7)),
+        scratch_shapes=[matrix, matrix]
+        + [blocks] * 9
+        + [matrix, matrix, piece, piece]
+        + [
+            pltpu.VMEM((SLOTS * HEAD_DIM, D), BF16),
+            pltpu.VMEM((4, 48, D), BF16),
+            dma((5, CHIPS)), dma((5, CHIPS)), dma((2, 4)), dma((2, 4)), dma((2, 4)),
+            dma((3, 4)), dma((3, 4)),
+        ],
+        compiler_params=params(3, 63),
+        name="feed",
+    )(middle, cot, halves, up_bias, gain, shift, down_bias, out_w, mixed)
+
+
+def back_kernel(
+    x, grad_mid, dq, dk, dv, hid, whole, gain,
+    grad_x, g_qkv, sums, head_sums,
+    joint, full, land, land_k, land_v, part, land_h,
+    send, recv, kv_send, kv_recv, g_send, g_recv,
+):
+    t, p, z = position()
+    greet(t, p, z)
+    swaps = []
+    for k in range(CHIPS):
+        other = (t + CHIPS - k) % CHIPS * 2 + 1 - p
+        mine = (t + CHIPS - k) % CHIPS
+        for j, (ref, dst) in enumerate(((dk, land_k), (dv, land_v))):
+            swaps.append(
+                to_twin(ref.at[other], dst.at[mine], kv_send.at[j, k], kv_recv.at[j, k], t, p, z)
+            )
+    for copy in swaps:
+        copy.start()
+    normed, inverse = normalize(x[...].astype(F32))
+    for copy in swaps:
+        copy.wait()
+    head_sums[...] = jnp.zeros_like(head_sums)
+
+    def block(k, carry):
+        dst = (t + k) % CHIPS
+        mine = dst * 2 + p
+        joint[dst, :, :WIDE] = dq[dst]
+        joint[dst, :, WIDE : 2 * WIDE] = (dk[mine].astype(F32) + land_k[dst].astype(F32)).astype(BF16)
+        low_v = (dv[mine].astype(F32) + land_v[dst].astype(F32)).astype(BF16)
+        joint[dst, :, 2 * WIDE :] = low_v
+        head_sums[0:1] += jnp.sum(dq[dst].astype(F32), 0, keepdims=True)
+        head_sums[1:2] += jnp.sum(low_v.astype(F32), 0, keepdims=True)
+        part[dst] = cols_product(joint[dst], whole[...]).astype(BF16)
+
+        to_chip(part.at[dst], land_h.at[t], send.at[k], recv.at[k], t, p, z, k).start()
+        return carry
+
+    lax.fori_loop(1, CHIPS, block, 0)
+    joint[t, :, :WIDE] = dq[t]
+    joint[t, :, WIDE : 2 * WIDE] = (dk[t * 2 + p].astype(F32) + land_k[t].astype(F32)).astype(BF16)
+    low_v = (dv[t * 2 + p].astype(F32) + land_v[t].astype(F32)).astype(BF16)
+    joint[t, :, 2 * WIDE :] = low_v
+    head_sums[0:1] += jnp.sum(dq[t].astype(F32), 0, keepdims=True)
+    head_sums[1:2] += jnp.sum(low_v.astype(F32), 0, keepdims=True)
+    total = cols_product(joint[t], whole[...])
+
+    def stack(ref):
+        return ref[...].reshape(CHIPS * ROWS, ref.shape[-1])
+
+    full[...] = rows_product(stack(hid), stack(joint)).astype(BF16)
+    swaps = [
+        to_twin(
+            full.at[rows16(i * 272 + (1 - p) * 128, 144)],
+            land.at[i],
+            g_send.at[i],
+            g_recv.at[i],
+            t,
+            p,
+            z,
+        )
+        for i in range(4)
+    ]
+    for copy in swaps:
+        copy.start()
+    for copy in swaps:
+        copy.wait()
+    for i in range(4):
+        own = full[rows16(i * 272 + p * 128, 144)].astype(F32)
+        g_qkv[i] = (own + land[i].astype(F32)).astype(BF16)
+    for k in range(1, CHIPS):
+        dst = (t + k) % CHIPS
+        to_chip(part.at[dst], land_h.at[t], send.at[k], recv.at[k], t, p, z, k).wait()
+        total = total + land_h[(t + CHIPS - k) % CHIPS].astype(F32)
+    grad_x[...] = grad_mid[...] + norm_back(total, normed, inverse, gain[...])
+    sums[0:1] = jnp.sum(total * normed, 0, keepdims=True)
+    sums[1:2] = jnp.sum(total, 0, keepdims=True)
+    sums[2:8] = jnp.zeros((6, D), F32)
+
+
+def back(x, grad_mid, dq, dk, dv, hid, whole, gain):
+    dma = pltpu.SemaphoreType.DMA
+    heads = pltpu.VMEM((CHIPS, ROWS, WIDE), BF16)
+    blocks = pltpu.VMEM((CHIPS, ROWS, D), BF16)
+    return pl.pallas_call(
+        back_kernel,
+        out_shape=(
+            jax.ShapeDtypeStruct((ROWS, D), F32),
+            jax.ShapeDtypeStruct((4, 144, 3 * WIDE), BF16),
+            jax.ShapeDtypeStruct((8, D), F32),
+            jax.ShapeDtypeStruct((8, WIDE), F32),
+        ),
+        in_specs=vmem(8),
+        out_specs=tuple(vmem(4)),
+        scratch_shapes=[
+            pltpu.VMEM((CHIPS, ROWS, 3 * WIDE), BF16),
+            pltpu.VMEM((D, 3 * WIDE), BF16),
+            pltpu.VMEM((4, 144, 3 * WIDE), BF16),
+            heads, heads, blocks, blocks,
+            dma((CHIPS,)), dma((CHIPS,)), dma((2, CHIPS)), dma((2, CHIPS)), dma((4,)), dma((4,)),
+        ],
+        compiler_params=params(4),
+        name="back",
+    )(x, grad_mid, dq, dk, dv, hid, whole, gain)
+
+
+def shares(array):
+    return lax.psum_scatter(array.reshape((-1, array.shape[-1])), "wsh", scatter_dimension=0, tiled=True)
+
+
+def joined(pieces, keep):
+    pairs = pieces.reshape(CHIPS, 2, keep, pieces.shape[-1])
+    return jnp.concatenate([pairs[:, 0], pairs[:, 1, 16:]], axis=1)
+
+
+def plane_device(
+    tokens, seq_lengths, cotangent, ln1_gain, ln1_bias, w_qkv, b_query, b_value, w_out, b_out,
+    ln2_gain, ln2_bias, w_up, b_up, w_down, b_down,
+):
+    c = lax.axis_index("ctx")
+    z = lax.axis_index("wsh")
+    t, p = (c // 2, c % 2)
+    x, cot, lengths = (tokens[0], cotangent[0], seq_lengths[0])
+    parity = p[None].astype(jnp.int32)
+    shard = D // 4
+    integers = functools.partial(jnp.arange, dtype=jnp.int32)
+
+    def columns_of(heads):
+        heads = jnp.concatenate([heads, jnp.full((1,), -40, jnp.int32)])
+        columns = jnp.repeat(heads, HEAD_DIM) * HEAD_DIM + integers(WIDE) % HEAD_DIM
+        return (integers(D)[:, None] == columns[None, :]).astype(BF16)
+
+    table = jnp.asarray(HEAD_TABLE, jnp.int32)
+    select = columns_of(lax.dynamic_index_in_dim(table, t, 0, keepdims=False))
+
+    vectors = jnp.stack(
+        [
+            b_query, b_value, b_out, b_down, ln1_gain, ln1_bias, ln2_gain, ln2_bias,
+            lax.dynamic_slice_in_dim(b_up, t * shard, shard),
+        ]
+    )
+    vectors = lax.all_gather(vectors, "wsh", axis=1, tiled=True)
+    head_bias = jnp.dot(vectors[:2], select, preferred_element_type=F32)
+    vectors = vectors.astype(F32)
+    bias_q, bias_v = (head_bias[0:1], head_bias[1:2])
+    bias_o, bias_d, gain_1, shift_1, gain_2, shift_2, bias_u = [
+        vectors[i : i + 1] for i in range(2, 9)
+    ]
+
+    qkv_rows = lax.dynamic_slice_in_dim(w_qkv, p * 128, 144, 0)
+    qkv_half = jnp.concatenate(
+        [
+            jnp.dot(qkv_rows[:, i * D : (i + 1) * D], select, preferred_element_type=F32)
+            for i in range(3)
+        ],
+        axis=1,
+    ).astype(BF16)
+    qkv_half = lax.all_gather(qkv_half, "wsh", axis=0)
+
+    ahead = jnp.asarray((0, 48, 32, 16), jnp.int32)[z]
+    i = p * 32 + integers(48)
+    early = jnp.where(i < HEAD_DIM, ahead + HEAD_DIM * t + i, -1)
+    late = jnp.where(i < ahead, i, 192 + i)
+    taken = jnp.where(t < CHIPS - 1, early, late)
+    pick = (taken[:, None] == integers(shard)[None, :]).astype(BF16)
+    out_half = jnp.dot(pick, w_out, preferred_element_type=F32).astype(BF16)
+    out_half = lax.all_gather(out_half, "wsh", axis=0)
+
+    up_rows = lax.dynamic_slice_in_dim(w_up, p * 128, 144, 0)
+    up_half = jnp.concatenate(
+        [lax.dynamic_slice_in_dim(up_rows, i * D + t * shard, shard, 1) for i in range(4)], axis=1
+    )
+    down_half = lax.dynamic_slice_in_dim(w_down, t * shard + p * 128, 144, 0)
+    halves = lax.all_gather(jnp.concatenate([up_half, down_half]), "wsh", axis=0)
+
+    q, k, v, hid, whole = project(x, qkv_half, gain_1, shift_1, bias_q, bias_v)
+    mixed, lse = attend(lengths, parity, q, k, v)
+    middle, out_w = out_project(x, mixed, out_half, bias_o)
+    output, grad_mid, grad_heads, g_out, g_feed, sums, up_sum = feed(
+        middle, cot, halves, bias_u, gain_2, shift_2, bias_d, out_w, mixed
+    )
+    feed_all = lax.all_gather(shares(g_feed), "ctx", axis=0)
+    out_all = lax.all_gather(shares(g_out), "ctx", axis=0)
+    dq, dk, dv = attend_back(lengths, parity, q, k, v, mixed, grad_heads, lse)
+    grad_x, g_qkv, sums_1, head_sums = back(x, grad_mid, dq, dk, dv, hid, whole, gain_1)
+    qkv_all = lax.all_gather(shares(g_qkv), "ctx", axis=0)
+
+    up_all = joined(feed_all[:, :144], 144)
+    grad_up = jnp.transpose(up_all.reshape(CHIPS, shard, 4, shard), (1, 2, 0, 3))
+    grad_up = grad_up.reshape(shard, 4 * D).astype(F32)
+    grad_down = joined(feed_all[:, 144:], 144).reshape(D, D).astype(F32)
+    row = integers(shard)
+    inner = row - ahead
+    source = jnp.where(
+        row < ahead,
+        240 + row,
+        jnp.where(inner < 192, inner // HEAD_DIM * 80 + inner % HEAD_DIM, 48 + row),
+    )
+    place = (source[:, None] == integers(320)[None, :]).astype(BF16)
+    grad_out = jnp.dot(place, joined(out_all, 48).reshape(320, D), preferred_element_type=F32)
+    selects = jnp.stack([columns_of(table[i]) for i in range(CHIPS)])
+    grad_qkv = jnp.concatenate(
+        [
+            lax.dot_general(
+                part, selects, (((0, 2), (0, 2)), ((), ())), preferred_element_type=F32
+            )
+            for part in jnp.split(joined(qkv_all, 144), 3, axis=2)
+        ],
+        axis=1,
+    )
+
+    head_vectors = lax.dot_general(
+        head_sums[:2],
+        select.astype(F32),
+        (((1,), (1,)), ((), ())),
+        precision=lax.Precision.HIGHEST,
+        preferred_element_type=F32,
+    )
+    ups = lax.dynamic_update_slice(
+        jnp.zeros((4, D), F32), up_sum.reshape(4, shard), (jnp.int32(0), t * shard)
+    )
+    totals = jnp.concatenate([sums[:4], sums_1[:2], head_vectors, ups])
+    totals = lax.psum(totals, ("ctx", "wsh"))
+    mine = lax.dynamic_slice_in_dim(totals, z * shard, shard, 1)
+    grad_b_up = lax.dynamic_index_in_dim(totals, 8 + z, 0, keepdims=False)
+    return (
+        output[None], grad_x[None],
+        mine[4], mine[5], grad_qkv, mine[6], mine[7], grad_out, mine[0],
+        mine[2], mine[3], grad_up, grad_b_up, grad_down, mine[1],
+    )
+
+
 def solution(mesh):
     in_specs = (
         P("wsh", "ctx", None),
@@ -375,6 +1238,8 @@
         P("wsh", None),
         P("wsh"),
     )
+    sizes = (mesh.shape["ctx"], mesh.shape["wsh"])
+    body = plane_device if sizes == (2 * CHIPS, 4) else on_device
     return jax.shard_map(
-        on_device, mesh=mesh, in_specs=in_specs, out_specs=out_specs, check_vma=False
-    )
+        body, mesh=mesh, in_specs=in_specs, out_specs=out_specs, check_vma=False
+    )

time: 1950 us -> 644 us (0.33)
  waiting for transfers between devices: 1550 us -> 104 us
  Pallas kernels: 0 us -> 336 us
  matrix products: 190 us -> 13.6 us
    reduce_scatter x4 -> x3, waiting for transfers between devices: 873 us -> 82.3 us  [shares(): lax.psum_scatter(array.reshape((-1, array.shape[-1])), 'wsh', scatter_dim...]
    all_gather x8 -> x4, waiting for transfers between devices: 540 us -> 20.1 us  [the longest x1 20.1 us: plane_device(): feed_all = lax.all_gather(shares(g_feed), 'ctx', axis=0)]
    pallas_call x0 -> x6, Pallas kernels: none -> 336 us  [the longest x1 143 us: feed(): pl.pallas_call(feed_kernel, out_shape=(jax.ShapeDtypeStruct((ROWS, D), BF...]
    dot_general x28 -> x10, matrix products: 190 us -> 13.6 us  [the longest x3 5.99 us: plane_device(): lax.dot_general(part, selects, (((0, 2), (0, 2)), ((), ())), preferred_el...]
    psum x1 -> x0, waiting for transfers between devices: 133 us -> none  [sectioned_sum(): return lax.psum(shares, 'ctx')]
    unnamed x2 -> x0, blocking collectives: 49.9 us -> none
    all_gather x2 -> x3, blocking collectives: 21.2 us -> 47.6 us  [the longest x1 20.5 us: plane_device(): out_half = lax.all_gather(out_half, 'wsh', axis=0)]
  transfers between devices with their start and end apart: 13 -> 7, of which waited for: 11 -> 3; matrix products, arithmetic and copies ran while one was open for 12% -> 5% of each run, Pallas kernels for 0% -> 18%
where the time goes in v1:
time: 644 us; the launch traced here: 637 us
  Pallas kernels  336 us (52%)
  waiting for transfers between devices  104 us (16%)
  blocking collectives  88.4 us (14%)
  local copies, waits for them, and re-layouts  66.9 us (10%)
  between operations  16 us (2%)
  matrix products  13.6 us (2%)
  other arithmetic  12.1 us (2%)
    pallas_call x1, Pallas kernels, feed(): pl.pallas_call(feed_kernel, out_shape=(jax.ShapeDtypeStruct((ROWS, D), BF...  143 us
    reduce_scatter x3, waiting for transfers between devices, shares(): lax.psum_scatter(array.reshape((-1, array.shape[-1])), 'wsh', scatter_dim...  82.3 us
    pallas_call x1, Pallas kernels, back(): pl.pallas_call(back_kernel, out_shape=(jax.ShapeDtypeStruct((ROWS, D), F3...  46.5 us
    pallas_call x1, Pallas kernels, out_project(): pl.pallas_call(out_kernel, out_shape=(jax.ShapeDtypeStruct((ROWS, D), F32...  41.7 us
    psum x1, blocking collectives, plane_device(): totals = lax.psum(totals, ('ctx', 'wsh'))  40.8 us
    pallas_call x1, Pallas kernels, project(): pl.pallas_call(project_kernel, out_shape=(blocks, keys, keys, jax.ShapeDt...  38.1 us
    pallas_call x1, Pallas kernels, attend_back(): pl.pallas_call(attend_back_kernel, out_shape=(jax.ShapeDtypeStruct((CHIPS...  33.6 us
    pallas_call x1, Pallas kernels, attend(): pl.pallas_call(attend_kernel, out_shape=(jax.ShapeDtypeStruct((CHIPS, ROW...  33 us
  transfers between devices with their start and end apart: 7, of which 3 were waited for; matrix products, arithmetic and copies ran while one was open for 5% of the time, Pallas kernels for 18%

profile of v1, /device:TPU:0, one launch (start us, length us, event | category | flops | bytes accessed | tf_op | source)
XLA Modules:
  0.0 636.8 jit_solution(313011011981133067)
XLA Ops:
  19.5 15.5 %all-gather.5 = bf16[4,272,9]{1,2,0:T(8,128)(2,1)S(1)} all-gather(bf16[1,272,9]{1,2,0:T(8,128)(2,1)S(1)} %bitcast.90), channel_id=1, replica_groups=mesh['ctx'=8,'wsh'=4] {'wsh'}, dimensions={0}, use_global_device_ids=true | all-gather | bytes 24480 | tf_op jit(solution)/shard_map/all_gather | solution.py:1114
  38.4 20.5 %all-gather = bf16[192,1088]{1,0:T(8,128)(2,1)} all-gather(bf16[48,1088]{1,0:T(8,128)(2,1)S(1)} %convolution_convert_fusion), channel_id=2, replica_groups=mesh['ctx'=8,'wsh'=4] {'wsh'}, dimensions={0}, use_global_device_ids=true | all-gather | bytes 522240 | tf_op jit(solution)/shard_map/all_gather | solution.py:1139
  60.5 38.1 %project.1 = (bf16[4,256,384]{2,1,0:T(8,128)(2,1)}, bf16[8,256,384]{2,1,0:T(8,128)(2,1)}, bf16[8,256,384]{2,1,0:T(8,128)(2,1)}, bf16[4,256,1088]{2,1,0:T(8,128)(2,1)}, bf16[1088,1152]{1,0:T(8,128)(2,1)}) custom-call(bf16[256,1088]{1,0:T(8,128)(2,1)} %bitcast.70, bf16[4,144,1152]{2,1,0:T(8,128)(2,1)} %all-gather.11.cloned.1.call-done.half, ...), custom_call_target="tpu_custom_call" | custom-call | tf_op jit(solution)/shard_map/project/pallas_call | solution.py:488
  102.6 33.0 %attend.1 = (bf16[4,256,384]{2,1,0:T(8,128)(2,1)S(1)}, f32[3,8,256]{2,1,0:T(8,128)S(1)}) custom-call(s32[5]{0:T(128)S(1)} %bitcast.64, s32[1]{0:T(128)} %bitcast.2.parity, bf16[4,256,384]{2,1,0:T(8,128)(2,1)S(1)} %copy-done.8, bf16[8,256,384]{2,1,0:T(8,128)(2,1)S(1)} %copy-done.6, bf16[8,256,384]{2,1,0:T(8,128)(2,1)S(1)} %copy-done.7), custom_call_target="tpu_custom_call" | custom-call | flops 4000000000 | bytes 5000000 | tf_op jit(solution)/shard_map/attend/pallas_call | solution.py:604
  136.5 41.7 %out_project.1 = (f32[256,1088]{1,0:T(8,128)}, bf16[384,1088]{1,0:T(8,128)(2,1)}) custom-call(bf16[256,1088]{1,0:T(8,128)(2,1)} %bitcast.71, bf16[4,256,384]{2,1,0:T(8,128)(2,1)} %copy-done.2, bf16[4,48,1088]{2,1,0:T(8,128)(2,1)} %bitcast.84, f32[1,1088]{1,0:T(1,128)} %get-tuple-element.139.bias), custom_call_target="tpu_custom_call" | custom-call | tf_op jit(solution)/shard_map/out_project/pallas_call | solution.py:762
  178.2 142.9 %feed.1 = (bf16[256,1088]{1,0:T(8,128)(2,1)}, f32[256,1088]{1,0:T(8,128)}, bf16[4,256,384]{2,1,0:T(8,128)(2,1)}, bf16[4,48,1088]{2,1,0:T(8,128)(2,1)}, bf16[4,28...) custom-call(f32[256,1088]{1,0:T(8,128)} %get-tuple-element.42.middle, bf16[256,1088]{1,0:T(8,128)(2,1)} %bitcast.83, ...), custom_call_target="tpu_custom_call" | custom-call | tf_op jit(solution)/shard_map/feed/pallas_call | solution.py:947
  323.4 33.6 %attend_back.1 = (bf16[4,256,384]{2,1,0:T(8,128)(2,1)S(1)}, bf16[8,256,384]{2,1,0:T(8,128)(2,1)S(1)}, bf16[8,256,384]{2,1,0:T(8,128)(2,1)}) custom-call(s32[5]{0:T(128)S(1)} %bitcast.65, s32[1]{0:T(128)} %bitcast.2.parity, bf16[4,256,384]{2,1,0:T(8,128)(2,1)S(1)} %copy-done.9, bf16[8,256,384]{2,1,0:T(8,128)(2,1)} %get-tuple-element.39.k, ...), custom_call_target="tpu_custom_call" | custom-call | flops 10000000000 | bytes 9000000 | tf_op jit(solution)/shard_map/attend_back/pallas_call | solution.py:697
  359.1 46.5 %back.1 = (f32[256,1088]{1,0:T(8,128)}, bf16[4,144,1152]{2,1,0:T(8,128)(2,1)}, f32[8,1088]{1,0:T(8,128)}, f32[8,384]{1,0:T(8,128)}) custom-call(bf16[256,1088]{1,0:T(8,128)(2,1)} %bitcast.72, f32[256,1088]{1,0:T(8,128)} %get-tuple-element.45.grad_mid, bf16[4,256,384]{2,1,0:T(8,128)(2,1)} %copy-done.5, bf16[8,256,384]{2,1,0:T(8,128)(2,1)} %copy-done.4, ...), custom_call_target="tpu_custom_call" | custom-call | tf_op jit(solution)/shard_map/back/pallas_call | solution.py:1057
  406.8 28.9 %reduce-scatter.4.cloned.1.call-done = bf16[144,1152]{1,0:T(8,128)(2,1)} async-done(((bf16[576,1152]{1,0:T(8,128)(2,1)}), bf16[144,1152]{1,0:T(8,128)(2,1)}) %reduce-scatter.4.cloned.1.call-update) | async-done | bytes 331792 | tf_op jit(solution)/shard_map/reduce_scatter | solution.py:1080
  436.0 53.4 %reduce-scatter.8.cloned.1.call-done = bf16[288,1088]{1,0:T(8,128)(2,1)} async-done(((bf16[1152,1088]{1,0:T(8,128)(2,1)}), bf16[288,1088]{1,0:T(8,128)(2,1)}) %reduce-scatter.8.cloned.1.call-update) | async-done | bytes 626704 | tf_op jit(solution)/shard_map/reduce_scatter | solution.py:1080
  497.2 40.8 %psum.7 = f32[12,1088]{1,0:T(8,128)S(1)} all-reduce(f32[12,1088]{1,0:T(8,128)S(1)} %pad_maximum_fusion.6), channel_id=1, replica_groups=mesh['ctx'=8,'wsh'=4] {'ctx','wsh'}, use_global_device_ids=true, to_apply=%region_0.1 | all-reduce | flops 13056 | bytes 104448 | tf_op jit(solution)/shard_map/psum | solution.py:1195
  539.3 11.6 %all-gather.3 = bf16[384,1088]{1,0:T(8,128)(2,1)S(1)} all-gather(bf16[48,1088]{1,0:T(8,128)(2,1)} %reduce-scatter.6.cloned.1.call-done), channel_id=5, replica_groups=mesh['ctx'=8,'wsh'=4] {'ctx'}, dimensions={0}, use_global_device_ids=true | all-gather | bytes 940032 | tf_op jit(solution)/shard_map/all_gather | solution.py:1155
  556.9 2.4 convolution_bitcast_fusion.2
  561.7 4.4 concatenate.74
  566.0 20.1 %all-gather.17.cloned.1.call-done = bf16[2304,1088]{1,0:T(8,128)(2,1)} async-done(((bf16[288,1088]{1,0:T(8,128)(2,1)}), bf16[2304,1088]{1,0:T(8,128)(2,1)}) %all-gather.17.cloned.1.call-update) | async-done | bytes 5013520 | tf_op jit(solution)/shard_map/all_gather | solution.py:1154
  586.2 4.5 fusion.49
  590.6 3.9 copy.63
  594.5 3.0 slice.168
  601.2 3.3 copy.65
  604.5 2.5 copy.69
  607.1 4.0 convert_bitcast_fusion
  611.1 7.1 %copy.66 = f32[272,4,4,272]{3,2,1,0:T(4,128)} copy(f32[272,4,4,272]{3,1,0,2:T(4,128)S(1)} %convert_bitcast_fusion) | data formatting | bytes 9469952 | tf_op jit(solution)/shard_map/convert_element_type | solution.py:1162
  618.2 8.3 %reshape.368 = f32[272,4352]{1,0:T(8,128)} reshape(f32[272,4,4,272]{3,2,1,0:T(4,128)} %copy.66) | data formatting | bytes 9469952 | tf_op jit(solution)/shard_map/convert_element_type | solution.py:1162
  626.7 2.8 bitcast_convert_fusion
  (166 shorter events, 48.0 us)
Async XLA Ops:
  7.2 30.9 %copy-start = (bf16[272,1088]{1,0:T(8,128)(2,1)S(1)}, bf16[272,1088]{1,0:T(8,128)(2,1)}, u32[]{:S(2)}) copy-start(bf16[272,1088]{1,0:T(8,128)(2,1)} %param.26) | copy-start | bytes 1775620
  7.2 53.3 %all-gather.11.cloned.1.call-start = ((), (), s32[]{:S(2)}) async-start(), calls=%async_computation.3 | async-start | bytes 1658880 | tf_op jit(solution)/shard_map/all_gather | solution.py:1130
  13.5 164.6 %all-gather.13.cloned.1.call-start = ((), (), s32[]{:S(2)}) async-start(), calls=%async_computation.7 | async-start | bytes 3317760 | tf_op jit(solution)/shard_map/all_gather | solution.py:1146
  16.4 18.7 %copy-start.17 = (bf16[1,256,1088]{1,2,0:T(8,128)(2,1)S(1)}, bf16[1,256,1088]{1,2,0:T(8,128)(2,1)}, u32[]{:S(2)}) copy-start(bf16[1,256,1088]{1,2,0:T(8,128)(2,1)} %param.20) | copy-start | bytes 1671172
  17.3 18.8 %copy-start.36 = (s32[4]{0:T(128)S(1)}, s32[4]{0:T(128)}, u32[]{:S(2)}) copy-start(s32[4]{0:T(128)} %constant.178.clone) | copy-start | bytes 52
  17.4 418.4 %reduce-scatter.4.cloned.1.call-start = ((), (), s32[]{:S(2)}) async-start(), calls=%async_computation.4 | async-start | bytes 1658880 | tf_op jit(solution)/shard_map/reduce_scatter | solution.py:1080
  38.4 60.2 %copy-start.11 = (s32[1,5]{1,0:T(1,128)S(1)}, s32[1,5]{1,0:T(1,128)}, u32[]{:S(2)}) copy-start(s32[1,5]{1,0:T(1,128)} %param.19) | copy-start | bytes 64
  178.2 143.0 %copy-start.3 = (bf16[4,256,384]{2,1,0:T(8,128)(2,1)S(1)}, bf16[4,256,384]{2,1,0:T(8,128)(2,1)}, u32[]{:S(2)}) copy-start(bf16[4,256,384]{2,1,0:T(8,128)(2,1)} %copy-done.2) | copy-start | bytes 2359300
  405.6 83.8 %reduce-scatter.8.cloned.1.call-start = ((), (), s32[]{:S(2)}) async-start(), calls=%async_computation.6 | async-start | bytes 3317760 | tf_op jit(solution)/shard_map/reduce_scatter | solution.py:1080
  405.6 83.8 %copy-start.34 = (s32[6]{0:T(128)S(1)}, s32[6]{0:T(128)}, u32[]{:S(2)}) copy-start(s32[6]{0:T(128)} %constant.197) | copy-start | bytes 76
  405.7 83.9 %copy-start.33 = (s32[6]{0:T(128)S(1)}, s32[6]{0:T(128)}, u32[]{:S(2)}) copy-start(s32[6]{0:T(128)} %constant.193) | copy-start | bytes 76
  405.7 84.1 %copy-start.32 = (s32[6]{0:T(128)S(1)}, s32[6]{0:T(128)}, u32[]{:S(2)}) copy-start(s32[6]{0:T(128)} %constant.189) | copy-start | bytes 76
  405.7 84.2 %copy-start.31 = (s32[6]{0:T(128)S(1)}, s32[6]{0:T(128)}, u32[]{:S(2)}) copy-start(s32[6]{0:T(128)} %constant.185) | copy-start | bytes 76
  406.2 86.5 %copy-start.15 = (bf16[256,1088]{1,0:T(8,128)(2,1)S(1)}, bf16[256,1088]{1,0:T(8,128)(2,1)}, u32[]{:S(2)}) copy-start(bf16[256,1088]{1,0:T(8,128)(2,1)} %get-tuple-element.44) | copy-start | bytes 1671172
  406.2 133.1 %reduce-scatter.6.cloned.1.call-start = ((), (), s32[]{:S(2)}) async-start(), calls=%async_computation.5 | async-start | bytes 552960 | tf_op jit(solution)/shard_map/reduce_scatter | solution.py:1080
  406.8 145.9 %all-gather.15.cloned.1.call-start = ((), (), s32[]{:S(2)}) async-start(), calls=%async_computation.8 | async-start | bytes 2985984 | tf_op jit(solution)/shard_map/all_gather | solution.py:1158
  435.8 150.4 %all-gather.17.cloned.1.call-start = ((), (), s32[]{:S(2)}) async-start(), calls=%async_computation.9 | async-start | bytes 5971968 | tf_op jit(solution)/shard_map/all_gather | solution.py:1154
  489.4 4.3 copy-start.14
  491.6 64.0 %copy-start.18 = (pred[1,1088,384]{2,1,0:T(32,128)(4,1)}, pred[1,1088,384]{2,1,0:T(32,128)(4,1)S(1)}, u32[]{:S(2)}) copy-start(pred[1,1088,384]{2,1,0:T(32,128)(4,1)S(1)} %iota_compare_fusion.2) | copy-start | bytes 1253380
  492.7 3.3 copy-start.21
  492.7 3.6 copy-start.35
  597.6 2.4 copy-start.12
  618.2 8.3 %copy-start.13 = (bf16[4,128,1088]{2,1,0:T(8,128)(2,1)S(1)}, bf16[4,128,1088]{2,1,0:T(8,128)(2,1)}, u32[]{:S(2)}) copy-start(bf16[4,128,1088]{2,1,0:T(8,128)(2,1)} %slice_bitcast_fusion.2) | copy-start | bytes 3342340
  626.7 2.8 copy-start.1
  (20 other events, 35.2 us)
Sparse Core Ops, SparseCore 0:
  13.6 42.1 all-gather.10
  58.0 54.4 all-gather.12
  405.7 29.9 reduce-scatter.3
  437.9 51.4 reduce-scatter.7
  491.5 20.7 reduce-scatter.5
  514.1 29.0 all-gather.14
  545.1 41.0 all-gather.16

commit v2 on v1

--- a/solution.py
+++ b/solution.py
@@ -345,51 +345,24 @@
 SLOTS = 5
 WIDE = 384
 ROWS = 256
+HALF = ROWS // 2
 CHIPS = 4
+TILE = 128
+FEED_ROWS = 304
 MESH_ID = pl.DeviceIdType.MESH
 F32, BF16 = (jnp.float32, jnp.bfloat16)
 NEG = -1e30
 HEAD_TABLE = ((0, 5, 9, 13, -40), (1, 6, 10, 14, -40), (2, 7, 11, 15, -40), (3, 4, 8, 12, 16))
+B_QUERY, B_VALUE, B_OUT, B_DOWN, GAIN_1, SHIFT_1, GAIN_2, SHIFT_2, B_UP = range(9)
 
 
 def nn(left, right):
     return jnp.dot(left, right, preferred_element_type=F32)
 
 
-def position():
-    c, z = (lax.axis_index("ctx"), lax.axis_index("wsh"))
-    return c // 2, c % 2, z
-
-
-def greet(t, p, z):
-    barrier = pltpu.get_barrier_semaphore()
-    for k in range(1, CHIPS):
-        pl.semaphore_signal(
-            barrier, inc=1, device_id=((t + k) % CHIPS * 2 + p, z), device_id_type=MESH_ID
-        )
-    pl.semaphore_signal(barrier, inc=1, device_id=(t * 2 + 1 - p, z), device_id_type=MESH_ID)
-    pl.semaphore_wait(barrier, CHIPS)
-
-
-def to_chip(src, dst, send, recv, t, p, z, k):
+def remote(src, dst, send, recv, where):
     return pltpu.make_async_remote_copy(
-        src_ref=src,
-        dst_ref=dst,
-        send_sem=send,
-        recv_sem=recv,
-        device_id=((t + k) % CHIPS * 2 + p, z),
-        device_id_type=MESH_ID,
-    )
-
-
-def to_twin(src, dst, send, recv, t, p, z):
-    return pltpu.make_async_remote_copy(
-        src_ref=src,
-        dst_ref=dst,
-        send_sem=send,
-        recv_sem=recv,
-        device_id=(t * 2 + 1 - p, z),
-        device_id_type=MESH_ID,
+        src_ref=src, dst_ref=dst, send_sem=send, recv_sem=recv, device_id=where, device_id_type=MESH_ID
     )
 
 
@@ -397,28 +370,214 @@
     return pl.ds(pl.multiple_of(start, 16), size)
 
 
-def weight_copies(half, whole, block, keep, step, local, send, recv, t, p, z, base=0):
-    copies = []
-    for i in range(4):
-        copies.append(
-            pltpu.make_async_copy(
-                half.at[i, rows16(base, keep)],
-                whole.at[rows16(i * block + p * step, keep)],
-                local.at[i],
-            )
+class Place:
+    def __init__(self):
+        self.c, self.z = (lax.axis_index("ctx"), lax.axis_index("wsh"))
+        self.t, self.p = (self.c // 2, self.c % 2)
+        self.tx, self.ty, self.td = (self.flip(1, 0), self.flip(0, 1), self.flip(1, 1))
+
+    def flip(self, dx, dy):
+        return (self.t // 2 + dy) % 2 * 2 + (self.t % 2 + dx) % 2
+
+    def chip(self, chip):
+        return (chip * 2 + self.p, self.z)
+
+    def twin(self):
+        return (self.t * 2 + 1 - self.p, self.z)
+
+    def plane(self, step):
+        return (self.c, (self.z + step) % 4)
+
+    def greet(self, planes=True):
+        barrier = pltpu.get_barrier_semaphore()
+        others = [self.chip(self.tx), self.chip(self.ty), self.twin()]
+        if planes:
+            others += [self.plane(1), self.plane(2), self.plane(3)]
+        for where in others:
+            pl.semaphore_signal(barrier, inc=1, device_id=where, device_id_type=MESH_ID)
+        pl.semaphore_wait(barrier, len(others))
+
+
+class Gather:
+    def __init__(self, e, own, view, rows, cut, send, recv):
+        self.e, self.own, self.view, self.send, self.recv = (e, own, view, send, recv)
+        self.parts = (pl.ds(0, cut), pl.ds(cut, rows - cut))
+
+    def copy(self, i):
+        e = self.e
+        chip = (e.t, e.t, e.t, e.t, e.tx, e.ty)[i]
+        part = self.parts[(0, 1, 1, 0, 0, 1)[i]]
+        src = self.own if i < 4 else self.view(chip)
+        where = e.chip((e.tx, e.tx, e.ty, e.ty, e.ty, e.tx)[i])
+        return remote(src.at[part], self.view(chip).at[part], self.send.at[i], self.recv.at[i], where)
+
+    def start(self):
+        for i in (0, 2, 1, 3):
+            self.copy(i).start()
+
+    def forward(self):
+        self.copy(0).wait_recv()
+        self.copy(4).start()
+        self.copy(2).wait_recv()
+        self.copy(5).start()
+
+    def have_x(self):
+        self.copy(1).wait_recv()
+
+    def have_y(self):
+        self.copy(3).wait_recv()
+
+    def have_far(self):
+        self.copy(4).wait_recv()
+        self.copy(5).wait_recv()
+
+    def sent(self):
+        for i in range(6):
+            self.copy(i).wait_send()
+
+
+class Scatter:
+    def __init__(self, e, part, land, send, recv):
+        self.e, self.part, self.land, self.send, self.recv = (e, part, land, send, recv)
+
+    def copy(self, i):
+        e = self.e
+        chip = (e.td, e.td, e.tx, e.tx, e.ty, e.ty)[i]
+        part = pl.ds((0, HALF, 0, HALF, HALF, 0)[i], HALF)
+        where = e.chip((e.tx, e.ty, e.tx, e.tx, e.ty, e.ty)[i])
+        return remote(
+            self.part.at[chip, part], self.land.at[i], self.send.at[i], self.recv.at[i], where
         )
-        copies.append(
-            to_twin(
-                half.at[i, rows16(base + p * (keep - step), step)],
-                whole.at[rows16(i * block + p * keep, step)],
-                send.at[i],
-                recv.at[i],
-                t,
-                p,
-                z,
-            )
+
+    def far_ready(self):
+        self.copy(0).start()
+        self.copy(1).start()
+
+    def x_ready(self):
+        self.copy(2).start()
+
+    def y_ready(self):
+        self.copy(4).start()
+
+    def relay(self):
+        self.copy(1).wait_recv()
+        chip = self.e.tx
+        self.part[chip, HALF:] = (self.part[chip, HALF:].astype(F32) + self.land[1].astype(F32)).astype(BF16)
+        self.copy(3).start()
+        self.copy(0).wait_recv()
+        chip = self.e.ty
+        self.part[chip, :HALF] = (self.part[chip, :HALF].astype(F32) + self.land[0].astype(F32)).astype(BF16)
+        self.copy(5).start()
+
+    def total(self):
+        for i in (2, 4, 3, 5):
+            self.copy(i).wait_recv()
+        first = self.land[2].astype(F32) + self.land[5].astype(F32)
+        second = self.land[4].astype(F32) + self.land[3].astype(F32)
+        return jnp.concatenate([first, second], 0)
+
+    def sent(self):
+        for i in range(6):
+            self.copy(i).wait_send()
+
+
+class ZGather:
+    def __init__(self, e, own, held, send, recv, put):
+        self.e, self.own, self.held, self.send, self.recv, self.put = (e, own, held, send, recv, put)
+
+    def copy(self, way, j):
+        e = self.e
+        shard = e.z - j if way == 0 else e.z + j
+        src = self.own if j == 0 else self.held.at[shard]
+        return remote(
+            src, self.held.at[shard], self.send.at[way, j], self.recv.at[way, j], e.plane(1 if way == 0 else 3)
         )
-    return copies
+
+    def sends(self, way, j):
+        z = self.e.z
+        return (z < 3) & (z >= j) if way == 0 else (z > 0) & (z <= 3 - j)
+
+    def step(self, j):
+        z = self.e.z
+        for way in range(2):
+            if j > 0:
+                @pl.when(z >= j if way == 0 else z <= 3 - j)
+                def _():
+                    self.copy(way, j - 1).wait_recv()
+            if j < 3:
+                @pl.when(self.sends(way, j))
+                def _():
+                    self.copy(way, j).start()
+            if j > 0:
+                @pl.when(z >= j if way == 0 else z <= 3 - j)
+                def _():
+                    self.put(z - j if way == 0 else z + j)
+
+    def sent(self):
+        for way in range(2):
+            for j in range(3):
+                @pl.when(self.sends(way, j))
+                def _():
+                    self.copy(way, j).wait_send()
+
+
+class ZScatter:
+    def __init__(self, e, own, staged, right, left, send, recv):
+        self.e, self.own, self.staged, self.land = (e, own, staged, (right, left))
+        self.send, self.recv = (send, recv)
+
+    def copy(self, way, j, src):
+        return remote(
+            src, self.land[way].at[j], self.send.at[way, j], self.recv.at[way, j],
+            self.e.plane(1 if way == 0 else 3),
+        )
+
+    def begin(self):
+        for plane, way in ((0, 0), (3, 1)):
+            @pl.when(self.e.z == plane)
+            def _():
+                for j in range(3):
+                    self.copy(way, j, self.own.at[3 - j if way == 0 else j]).start()
+
+    def relay(self, way, j):
+        dest = 3 - j if way == 0 else j
+        self.copy(way, j, self.staged.at[dest]).wait_recv()
+        self.staged[dest] = (self.own[dest].astype(F32) + self.land[way][j].astype(F32)).astype(BF16)
+        self.copy(way, j, self.staged.at[dest]).start()
+
+    def first(self):
+        for plane, way in ((1, 0), (2, 1)):
+            @pl.when(self.e.z == plane)
+            def _():
+                self.relay(way, 0)
+
+    def second(self):
+        for plane, way in ((1, 0), (2, 1)):
+            @pl.when(self.e.z == plane)
+            def _():
+                self.relay(1 - way, 0)
+                self.relay(way, 1)
+
+    def last(self, out):
+        right, left = self.land
+        for z in range(4):
+            @pl.when(self.e.z == z)
+            def _():
+                total = self.own[z].astype(F32)
+                if z > 0:
+                    self.copy(0, 3 - z, self.own.at[z]).wait_recv()
+                    total = total + right[3 - z].astype(F32)
+                if z < 3:
+                    self.copy(1, z, self.own.at[z]).wait_recv()
+                    total = total + left[z].astype(F32)
+                out[...] = total.astype(BF16)
+                for way in range(2):
+                    for j in range((3 - z) if way == 0 else z):
+                        self.copy(way, j, self.own.at[z]).wait_send()
+
+
+def dma(*shape):
+    return pltpu.SemaphoreType.DMA(shape)
 
 
 def params(number, mib=56):
@@ -431,76 +590,165 @@
     return [pl.BlockSpec(memory_space=pltpu.VMEM)] * count
 
 
+class Halves:
+    def __init__(self, e, whole, block, keep, step, local, send, recv):
+        self.e, self.whole, self.block, self.keep, self.step = (e, whole, block, keep, step)
+        self.local, self.send, self.recv = (local, send, recv)
+
+    def copies(self, src, shard):
+        e = self.e
+        return (
+            pltpu.make_async_copy(
+                src, self.whole.at[rows16(shard * self.block + e.p * self.step, self.keep)], self.local.at[shard]
+            ),
+            remote(
+                src.at[rows16(e.p * (self.keep - self.step), self.step)],
+                self.whole.at[rows16(shard * self.block + e.p * self.keep, self.step)],
+                self.send.at[shard], self.recv.at[shard], e.twin(),
+            ),
+        )
+
+    def put(self, src, shard):
+        for copy in self.copies(src, shard):
+            copy.start()
+
+    def wait(self, src):
+        for shard in range(4):
+            for copy in self.copies(src, shard):
+                copy.wait()
+
+
 def project_kernel(
-    x, half, gain, shift, bias_q, bias_v,
-    q_out, k_out, v_out, h_out, whole,
-    send, recv, w_local, w_send, w_recv, kv_send, kv_recv,
+    x, cot, half, half_o, vec_in, select,
+    q_out, k_out, v_out, h_out, cots, whole, out_w, vecs,
+    held, held_o, raw, vec_land,
+    v_send, v_recv, z_send, z_recv, a_send, a_recv, w_local, w_send, w_recv, kv_send, kv_recv,
 ):
-    t, p, z = position()
-    greet(t, p, z)
-    weights = weight_copies(half, whole, 272, 144, 128, w_local, w_send, w_recv, t, p, z)
-    for copy in weights:
+    e = Place()
+    t, p, z = (e.t, e.p, e.z)
+    e.greet()
+    vectors = [
+        remote(vec_in, vec_land.at[k], v_send.at[k], v_recv.at[k], e.plane(k)) for k in range(1, 4)
+    ]
+    for copy in vectors:
         copy.start()
+    into = Halves(e, whole, 272, 144, 128, w_local.at[0], w_send.at[0], w_recv.at[0])
+    into_o = Halves(e, raw, 80, 48, 32, w_local.at[1], w_send.at[1], w_recv.at[1])
+    chain = ZGather(
+        e, half, held, z_send.at[0], z_recv.at[0], lambda shard: into.put(held.at[shard], shard)
+    )
+    chain_o = ZGather(
+        e, half_o, held_o, z_send.at[1], z_recv.at[1], lambda shard: into_o.put(held_o.at[shard], shard)
+    )
+    chain.step(0)
+    into.put(half, z)
     normed, _ = normalize(x[...].astype(F32))
-    h_out[t] = (normed * gain[...] + shift[...]).astype(BF16)
-    sends = [
-        to_chip(h_out.at[t], h_out.at[t], send.at[k], recv.at[k], t, p, z, k)
-        for k in range(1, CHIPS)
-    ]
-    for copy in sends:
-        copy.start()
-    for copy in weights:
-        copy.wait()
+    total = vec_in[...].astype(F32)
+    for k in range(1, 4):
+        vectors[k - 1].wait_recv()
+        total = total + vec_land[k].astype(F32)
+    vecs[...] = total
+    h_out[t] = (normed * vecs[GAIN_1 : GAIN_1 + 1] + vecs[SHIFT_1 : SHIFT_1 + 1]).astype(BF16)
+    hidden = Gather(e, h_out.at[t], lambda chip: h_out.at[chip], ROWS, HALF, a_send.at[0], a_recv.at[0])
+    hidden.start()
+    bias = nn(total.astype(BF16), select[...])
+    bias_q, bias_v = (bias[B_QUERY : B_QUERY + 1], bias[B_VALUE : B_VALUE + 1])
+    cots[t] = cot[...]
+    chain.step(1)
+    hidden.forward()
+    tops = Gather(e, cot, lambda chip: cots.at[chip], ROWS, HALF, a_send.at[1], a_recv.at[1])
+    tops.start()
+    chain.step(2)
+    chain_o.step(0)
+    into_o.put(half_o, z)
+    chain.step(3)
+    into.wait(half)
 
     def block(k, carry):
-        src = (t + CHIPS - k) % CHIPS
-
-        @pl.when(k > 0)
-        def _():
-            to_chip(h_out.at[src], h_out.at[src], send.at[k], recv.at[k], t, p, z, 0 * k + 1).wait_recv()
+        src = e.flip((k + 1) // 2 % 2, k // 2)
+
+        @pl.when(k == 1)
+        def _():
+            hidden.have_x()
+
+        @pl.when(k == 2)
+        def _():
+            hidden.have_far()
+
+        @pl.when(k == 3)
+        def _():
+            hidden.have_y()
 
         h = h_out[src]
-        q_out[src] = ((nn(h, whole[:, :WIDE]) + bias_q[...]).astype(BF16) * 0.125).astype(BF16)
+        q_out[src] = ((nn(h, whole[:, :WIDE]) + bias_q).astype(BF16) * 0.125).astype(BF16)
         mine = src * 2 + p
         k_out[mine] = nn(h, whole[:, WIDE : 2 * WIDE]).astype(BF16)
-        to_twin(k_out.at[mine], k_out.at[mine], kv_send.at[k], kv_recv.at[k], t, p, z).start()
-        v_out[mine] = (nn(h, whole[:, 2 * WIDE :]) + bias_v[...]).astype(BF16)
-        to_twin(
-            v_out.at[mine], v_out.at[mine], kv_send.at[k + CHIPS], kv_recv.at[k + CHIPS], t, p, z
+        remote(k_out.at[mine], k_out.at[mine], kv_send.at[k], kv_recv.at[k], e.twin()).start()
+        v_out[mine] = (nn(h, whole[:, 2 * WIDE :]) + bias_v).astype(BF16)
+        remote(
+            v_out.at[mine], v_out.at[mine], kv_send.at[k + CHIPS], kv_recv.at[k + CHIPS], e.twin()
         ).start()
         return carry
 
     lax.fori_loop(0, CHIPS, block, 0)
-    for copy in sends:
+    chain_o.step(1)
+    tops.forward()
+    chain_o.step(2)
+    chain_o.step(3)
+    into_o.wait(half_o)
+
+    @pl.when(t == CHIPS - 1)
+    def _():
+        out_w[: SLOTS * HEAD_DIM] = raw[...]
+
+    @pl.when(t < CHIPS - 1)
+    def _():
+        for i in range(4):
+            out_w[i * HEAD_DIM : (i + 1) * HEAD_DIM] = raw[i * 80 : i * 80 + HEAD_DIM]
+        out_w[4 * HEAD_DIM : 5 * HEAD_DIM] = jnp.zeros((HEAD_DIM, D), BF16)
+
+    out_w[SLOTS * HEAD_DIM :] = jnp.zeros((WIDE - SLOTS * HEAD_DIM, D), BF16)
+    for k in range(CHIPS):
+        src = e.flip((k + 1) // 2 % 2, k // 2)
+        other = src * 2 + 1 - p
+        mine = src * 2 + p
+        for ref, j in ((k_out, k), (v_out, k + CHIPS)):
+            remote(ref.at[mine], ref.at[mine], kv_send.at[j], kv_recv.at[j], e.twin()).wait_send()
+            remote(ref.at[other], ref.at[other], kv_send.at[j], kv_recv.at[j], e.twin()).wait_recv()
+    tops.have_x()
+    tops.have_y()
+    tops.have_far()
+    for user in (hidden, tops, chain, chain_o):
+        user.sent()
+    for copy in vectors:
         copy.wait_send()
-    for k in range(CHIPS):
-        other = (t + CHIPS - k) % CHIPS * 2 + 1 - p
-        mine = (t + CHIPS - k) % CHIPS * 2 + p
-        for ref, j in ((k_out, k), (v_out, k + CHIPS)):
-            to_twin(ref.at[mine], ref.at[mine], kv_send.at[j], kv_recv.at[j], t, p, z).wait_send()
-            to_twin(ref.at[other], ref.at[other], kv_send.at[j], kv_recv.at[j], t, p, z).wait_recv()
-
-
-def project(x, half, gain, shift, bias_q, bias_v):
+
+
+def project(x, cot, half, half_o, vec_in, select):
     blocks = jax.ShapeDtypeStruct((CHIPS, ROWS, WIDE), BF16)
     keys = jax.ShapeDtypeStruct((2 * CHIPS, ROWS, WIDE), BF16)
-    dma = pltpu.SemaphoreType.DMA
+    rows = jax.ShapeDtypeStruct((CHIPS, ROWS, D), BF16)
     return pl.pallas_call(
         project_kernel,
         out_shape=(
-            blocks, keys, keys,
-            jax.ShapeDtypeStruct((CHIPS, ROWS, D), BF16),
+            blocks, keys, keys, rows, rows,
             jax.ShapeDtypeStruct((D, 3 * WIDE), BF16),
+            jax.ShapeDtypeStruct((WIDE, D), BF16),
+            jax.ShapeDtypeStruct((16, D), F32),
         ),
         in_specs=vmem(6),
-        out_specs=tuple(vmem(5)),
+        out_specs=tuple(vmem(8)),
         scratch_shapes=[
-            dma((CHIPS,)), dma((CHIPS,)), dma((4,)), dma((4,)), dma((4,)),
-            dma((2 * CHIPS,)), dma((2 * CHIPS,)),
+            pltpu.VMEM((4, 144, 3 * WIDE), BF16),
+            pltpu.VMEM((4, 48, D), BF16),
+            pltpu.VMEM((SLOTS * HEAD_DIM, D), BF16),
+            pltpu.VMEM((4, 16, D), BF16),
+            dma(4), dma(4), dma(2, 2, 3), dma(2, 2, 3), dma(2, 6), dma(2, 6),
+            dma(2, 4), dma(2, 4), dma(2, 4), dma(2 * CHIPS), dma(2 * CHIPS),
         ],
         compiler_params=params(1),
         name="project",
-    )(x, half, gain, shift, bias_q, bias_v)
+    )(x, cot, half, half_o, vec_in, select)
 
 
 def tile_bounds(lengths, block):
@@ -721,123 +969,126 @@
     )(lengths, parity, q, k, v, mixed, grad, lse)
 
 
-def out_kernel(
-    x, mixed, half, bias, middle, whole, raw, parts, landed, send, recv, w_local, w_send, w_recv
-):
-    t, p, z = position()
-    greet(t, p, z)
-    weights = weight_copies(half, raw, 80, 48, 32, w_local, w_send, w_recv, t, p, z)
-    for copy in weights:
-        copy.start()
-    for copy in weights:
-        copy.wait()
-
-    @pl.when(t == CHIPS - 1)
-    def _():
-        whole[: SLOTS * HEAD_DIM] = raw[...]
-
-    @pl.when(t < CHIPS - 1)
-    def _():
-        for i in range(4):
-            whole[i * HEAD_DIM : (i + 1) * HEAD_DIM] = raw[i * 80 : i * 80 + HEAD_DIM]
-        whole[4 * HEAD_DIM : 5 * HEAD_DIM] = jnp.zeros((HEAD_DIM, D), BF16)
-
-    whole[SLOTS * HEAD_DIM :] = jnp.zeros((WIDE - SLOTS * HEAD_DIM, D), BF16)
-
-    def part(k, carry):
-        parts[k] = nn(mixed[(t + k) % CHIPS], whole[...]).astype(BF16)
-        to_chip(parts.at[k], landed.at[k], send.at[k], recv.at[k], t, p, z, k).start()
+def out_kernel(x, mixed, whole, vecs, middle, part, land, send, recv):
+    e = Place()
+    e.greet(planes=False)
+    sums = Scatter(e, part, land, send, recv)
+
+    def block(k, carry):
+        dest = e.flip(1 - k // 2, 1 - k % 2)
+        part[dest] = nn(mixed[dest], whole[...]).astype(BF16)
+
+        @pl.when(k == 0)
+        def _():
+            sums.far_ready()
+
+        @pl.when(k == 1)
+        def _():
+            sums.x_ready()
+
+        @pl.when(k == 2)
+        def _():
+            sums.y_ready()
+
         return carry
 
-    lax.fori_loop(1, CHIPS, part, 0)
-    total = x[...].astype(F32) + bias[...] + nn(mixed[t], whole[...])
-    for k in range(1, CHIPS):
-        to_chip(parts.at[k], landed.at[k], send.at[k], recv.at[k], t, p, z, k).wait()
-        total = total + landed[k].astype(F32)
-    middle[...] = total
-
-
-def out_project(x, mixed, half, bias):
-    dma = pltpu.SemaphoreType.DMA
+    lax.fori_loop(0, CHIPS - 1, block, 0)
+    total = x[...].astype(F32) + vecs[B_OUT : B_OUT + 1] + nn(mixed[e.t], whole[...])
+    sums.relay()
+    middle[...] = total + sums.total()
+    sums.sent()
+
+
+def out_project(x, mixed, whole, vecs):
     return pl.pallas_call(
         out_kernel,
-        out_shape=(
-            jax.ShapeDtypeStruct((ROWS, D), F32),
-            jax.ShapeDtypeStruct((WIDE, D), BF16),
-        ),
+        out_shape=jax.ShapeDtypeStruct((ROWS, D), F32),
         in_specs=vmem(4),
-        out_specs=tuple(vmem(2)),
+        out_specs=vmem(1)[0],
         scratch_shapes=[
-            pltpu.VMEM((SLOTS * HEAD_DIM, D), BF16),
             pltpu.VMEM((CHIPS, ROWS, D), BF16),
-            pltpu.VMEM((CHIPS, ROWS, D), BF16),
-            dma((CHIPS,)), dma((CHIPS,)), dma((4,)), dma((4,)), dma((4,)),
+            pltpu.VMEM((6, HALF, D), BF16),
+            dma(6), dma(6),
         ],
         compiler_params=params(2),
         name="out_project",
-    )(x, mixed, half, bias)
+    )(x, mixed, whole, vecs)
 
 
 def feed_kernel(
-    middle, cot, halves, up_bias, gain, shift, down_bias, out_w, mixed,
-    output, grad_mid, gh_heads, g_out, g_feed, sums, up_sum,
-    up, down, hid, cots, act, gpre, part_o, part_h, land_o, land_h, gmid, full_up, full_down, land_up, land_down, raw, land_out,
-    send, recv, w_local, w_send, w_recv, g_send, g_recv,
+    middle, cots, halves, vecs, out_w, mixed,
+    output, grad_mid, gh_heads, g_out, share, sums, up_sum,
+    up, down, hid, act, gpre, part_o, part_h, gmid, sum_o_land, sum_h_land,
+    full_up, full_down, land_up, land_down, land_more, g_feed, staged, z_right, z_left, raw, land_out,
+    a_send, a_recv, s_send, s_recv, w_local, w_send, w_recv, d_local, d_send, d_recv, g_send, g_recv, z_send, z_recv,
 ):
-    t, p, z = position()
-    greet(t, p, z)
-    weights = weight_copies(
-        halves, up, 272, 144, 128, w_local.at[0], w_send.at[0], w_recv.at[0], t, p, z
-    ) + weight_copies(
-        halves, down, 272, 144, 128, w_local.at[1], w_send.at[1], w_recv.at[1], t, p, z, 144
-    )
-    normed, inverse = normalize(middle[...])
-    hid[t] = (normed * gain[...] + shift[...]).astype(BF16)
-    cots[t] = cot[...]
-    for k in range(1, CHIPS):
-        to_chip(hid.at[t], hid.at[t], send.at[0, k], recv.at[0, k], t, p, z, k).start()
+    e = Place()
+    t, p = (e.t, e.p)
+    e.greet()
+    into = Halves(e, up, 272, 144, 128, w_local, w_send, w_recv)
+    weights = []
+    for i in range(4):
+        weights.extend(into.copies(halves.at[i, pl.ds(0, 144)], i))
+    for i in range(5):
+        src = halves.at[i, pl.ds(144, TILE)] if i < 4 else halves.at[t, pl.ds(272, 32)]
+        dst = down.at[rows16(256 * i + p * TILE, TILE) if i < 4 else rows16(1024 + p * 32, 32)]
+        weights.append(pltpu.make_async_copy(src, dst, d_local.at[i]))
+        weights.append(remote(src, dst, d_send.at[i], d_recv.at[i], e.twin()))
     for copy in weights:
         copy.start()
-    for k in range(1, CHIPS):
-        to_chip(cots.at[t], cots.at[t], send.at[1, k], recv.at[1, k], t, p, z, k).start()
+    normed, inverse = normalize(middle[...])
+    hid[t] = (normed * vecs[GAIN_2 : GAIN_2 + 1] + vecs[SHIFT_2 : SHIFT_2 + 1]).astype(BF16)
+    hidden = Gather(e, hid.at[t], lambda chip: hid.at[chip], ROWS, HALF, a_send.at[0], a_recv.at[0])
+    hidden.start()
+    sum_h = Scatter(e, part_h, sum_h_land, s_send.at[0], s_recv.at[0])
+    sum_o = Scatter(e, part_o, sum_o_land, s_send.at[1], s_recv.at[1])
     for copy in weights:
         copy.wait()
     up_sum[...] = jnp.zeros_like(up_sum)
 
     def block(k, carry):
-        src = (t + CHIPS - k) % CHIPS
-
-        @pl.when(k > 0)
-        def _():
-            to_chip(hid.at[src], hid.at[src], send.at[0, k], recv.at[0, k], t, p, z, 1).wait_recv()
-
-        pre = nn(hid[src], up[...]) + up_bias[...]
+        src = e.flip((k + 1) // 2 % 2, k // 2)
+
+        @pl.when(k == 1)
+        def _():
+            hidden.forward()
+            hidden.have_x()
+
+        @pl.when(k == 2)
+        def _():
+            hidden.have_far()
+
+        @pl.when(k == 3)
+        def _():
+            hidden.have_y()
+
+        pre = nn(hid[src], up[...]) + vecs[B_UP : B_UP + 1]
         cdf = 0.5 * (1.0 + lax.erf(pre * math.sqrt(0.5)))
         slope = cdf + pre * (jnp.exp(-0.5 * pre * pre) * (1.0 / math.sqrt(2.0 * math.pi)))
         act[src] = (pre * cdf).astype(BF16)
-
-        @pl.when(k > 0)
-        def _():
-            to_chip(cots.at[src], cots.at[src], send.at[1, k], recv.at[1, k], t, p, z, 1).wait_recv()
-
         grad = cols_product(cots[src], down[...]) * slope
         low = grad.astype(BF16)
         gpre[src] = low
         up_sum[...] += jnp.sum(low.astype(F32), 0, keepdims=True)
         part_h[src] = cols_product(low, up[...]).astype(BF16)
 
-        @pl.when(k > 0)
-        def _():
-            to_chip(part_h.at[src], land_h.at[t], send.at[2, k], recv.at[2, k], t, p, z, CHIPS - k).start()
+        @pl.when(k == 1)
+        def _():
+            sum_h.x_ready()
+
+        @pl.when(k == 2)
+        def _():
+            sum_h.far_ready()
+
+        @pl.when(k == 3)
+        def _():
+            sum_h.y_ready()
 
         part_o[src] = nn(act[src], down[...]).astype(BF16)
         return carry
 
     lax.fori_loop(0, CHIPS, block, 0)
-
-    for k in range(1, CHIPS):
-        src = (t + CHIPS - k) % CHIPS
-        to_chip(part_o.at[src], land_o.at[t], send.at[3, k], recv.at[3, k], t, p, z, CHIPS - k).start()
+    sum_h.relay()
 
     def stack(ref):
         return ref[...].reshape(CHIPS * ROWS, ref.shape[-1])
@@ -846,32 +1097,34 @@
     full_down[...] = rows_product(stack(act), stack(cots)).astype(BF16)
     swaps = []
     for i in range(4):
-        for j, (full, land) in enumerate(((full_up, land_up), (full_down, land_down))):
-            swaps.append(
-                to_twin(
-                    full.at[rows16(i * 272 + (1 - p) * 128, 144)],
-                    land.at[i],
-                    g_send.at[j, i],
-                    g_recv.at[j, i],
-                    t,
-                    p,
-                    z,
-                )
+        swaps.append(
+            remote(
+                full_up.at[rows16(i * 272 + (1 - p) * TILE, 144)], land_up.at[i],
+                g_send.at[0, i], g_recv.at[0, i], e.twin(),
             )
+        )
+        swaps.append(
+            remote(
+                full_down.at[rows16(256 * i + (1 - p) * TILE, TILE)], land_down.at[i],
+                g_send.at[1, i], g_recv.at[1, i], e.twin(),
+            )
+        )
+    swaps.append(
+        remote(
+            full_down.at[rows16(1024 + (1 - p) * 32, 32)], land_more, g_send.at[2, 0], g_recv.at[2, 0], e.twin()
+        )
+    )
     for copy in swaps:
         copy.start()
 
-    total = part_h[t].astype(F32)
-    for k in range(1, CHIPS):
-        to_chip(part_h.at[t], land_h.at[t], send.at[2, k], recv.at[2, k], t, p, z, k).wait()
-        total = total + land_h[(t + k) % CHIPS].astype(F32)
-    top = cot[...].astype(F32)
-    grad_middle = top + norm_back(total, normed, inverse, gain[...])
+    total = part_h[t].astype(F32) + sum_h.total()
+    top = cots[t].astype(F32)
+    grad_middle = top + norm_back(total, normed, inverse, vecs[GAIN_2 : GAIN_2 + 1])
     grad_mid[...] = grad_middle
     low = grad_middle.astype(BF16)
     gmid[t] = low
-    for k in range(1, CHIPS):
-        to_chip(gmid.at[t], gmid.at[t], send.at[4, k], recv.at[4, k], t, p, z, k).start()
+    spread = Gather(e, gmid.at[t], lambda chip: gmid.at[chip], ROWS, HALF, a_send.at[1], a_recv.at[1])
+    spread.start()
     sums[0:1] = jnp.sum(low.astype(F32), 0, keepdims=True)
     sums[1:2] = jnp.sum(top, 0, keepdims=True)
     sums[2:3] = jnp.sum(total * normed, 0, keepdims=True)
@@ -880,22 +1133,40 @@
 
     for copy in swaps:
         copy.wait()
+    more = (full_down[rows16(1024 + p * 32, 32)].astype(F32) + land_more[...].astype(F32)).astype(BF16)
     for i in range(4):
-        for j, (full, land) in enumerate(((full_up, land_up), (full_down, land_down))):
-            own = full[rows16(i * 272 + p * 128, 144)].astype(F32)
-            g_feed[i, j * 144 : (j + 1) * 144] = (own + land[i].astype(F32)).astype(BF16)
+        own = full_up[rows16(i * 272 + p * TILE, 144)].astype(F32)
+        g_feed[i, :144] = (own + land_up[i].astype(F32)).astype(BF16)
+        own = full_down[rows16(256 * i + p * TILE, TILE)].astype(F32)
+        g_feed[i, 144:272] = (own + land_down[i].astype(F32)).astype(BF16)
+        g_feed[i, 272:] = more
+    planes = ZScatter(e, g_feed, staged, z_right, z_left, z_send, z_recv)
+    planes.begin()
+    spread.forward()
+    sum_o.far_ready()
+    sum_o.x_ready()
+    sum_o.y_ready()
 
     def heads(k, carry):
-        src = (t + CHIPS - k) % CHIPS
-
-        @pl.when(k > 0)
-        def _():
-            to_chip(gmid.at[src], gmid.at[src], send.at[4, k], recv.at[4, k], t, p, z, 1).wait_recv()
+        src = e.flip((k + 1) // 2 % 2, k // 2)
+
+        @pl.when(k == 1)
+        def _():
+            spread.have_x()
+
+        @pl.when(k == 2)
+        def _():
+            spread.have_far()
+
+        @pl.when(k == 3)
+        def _():
+            spread.have_y()
 
         gh_heads[src] = cols_product(gmid[src], out_w[...]).astype(BF16)
         return carry
 
     lax.fori_loop(0, CHIPS, heads, 0)
+    planes.first()
     grad_out = rows_product(stack(mixed), stack(gmid)).astype(BF16)
 
     @pl.when(t == CHIPS - 1)
@@ -909,41 +1180,31 @@
             raw[i * 80 + HEAD_DIM : (i + 1) * 80] = jnp.zeros((16, D), BF16)
 
     swaps = [
-        to_twin(
-            raw.at[rows16(i * 80 + (1 - p) * 32, 48)],
-            land_out.at[i],
-            g_send.at[2, i],
-            g_recv.at[2, i],
-            t,
-            p,
-            z,
+        remote(
+            raw.at[rows16(i * 80 + (1 - p) * 32, 48)], land_out.at[i], g_send.at[3, i], g_recv.at[3, i], e.twin()
         )
         for i in range(4)
     ]
     for copy in swaps:
         copy.start()
+    sum_o.relay()
     for copy in swaps:
         copy.wait()
     for i in range(4):
         own = raw[rows16(i * 80 + p * 32, 48)].astype(F32)
         g_out[i] = (own + land_out[i].astype(F32)).astype(BF16)
-
-    result = middle[...] + down_bias[...] + part_o[t].astype(F32)
-    for k in range(1, CHIPS):
-        to_chip(part_o.at[t], land_o.at[t], send.at[3, k], recv.at[3, k], t, p, z, k).wait()
-        result = result + land_o[(t + k) % CHIPS].astype(F32)
-    output[...] = result.astype(BF16)
-    for k in range(1, CHIPS):
-        to_chip(hid.at[t], hid.at[t], send.at[0, k], recv.at[0, k], t, p, z, k).wait_send()
-        to_chip(cots.at[t], cots.at[t], send.at[1, k], recv.at[1, k], t, p, z, k).wait_send()
-        to_chip(gmid.at[t], gmid.at[t], send.at[4, k], recv.at[4, k], t, p, z, k).wait_send()
-
-
-def feed(middle, cot, halves, up_bias, gain, shift, down_bias, out_w, mixed):
-    dma = pltpu.SemaphoreType.DMA
+    planes.second()
+    result = middle[...] + vecs[B_DOWN : B_DOWN + 1] + part_o[t].astype(F32)
+    output[...] = (result + sum_o.total()).astype(BF16)
+    planes.last(share)
+    for user in (hidden, spread, sum_h, sum_o):
+        user.sent()
+
+
+def feed(middle, cots, halves, vecs, out_w, mixed):
     blocks = pltpu.VMEM((CHIPS, ROWS, D), BF16)
+    lands = pltpu.VMEM((6, HALF, D), BF16)
     matrix = pltpu.VMEM((D, D), BF16)
-    piece = pltpu.VMEM((4, 144, D), BF16)
     return pl.pallas_call(
         feed_kernel,
         out_shape=(
@@ -951,138 +1212,300 @@
             jax.ShapeDtypeStruct((ROWS, D), F32),
             jax.ShapeDtypeStruct((CHIPS, ROWS, WIDE), BF16),
             jax.ShapeDtypeStruct((4, 48, D), BF16),
-            jax.ShapeDtypeStruct((4, 288, D), BF16),
+            jax.ShapeDtypeStruct((FEED_ROWS, D), BF16),
             jax.ShapeDtypeStruct((8, D), F32),
             jax.ShapeDtypeStruct((1, D), F32),
         ),
-        in_specs=vmem(9),
+        in_specs=vmem(6),
         out_specs=tuple(vmem(7)),
         scratch_shapes=[matrix, matrix]
-        + [blocks] * 9
-        + [matrix, matrix, piece, piece]
+        + [blocks] * 6
+        + [lands, lands, matrix, matrix]
         + [
+            pltpu.VMEM((4, 144, D), BF16),
+            pltpu.VMEM((4, TILE, D), BF16),
+            pltpu.VMEM((32, D), BF16),
+            pltpu.VMEM((4, FEED_ROWS, D), BF16),
+            pltpu.VMEM((4, FEED_ROWS, D), BF16),
+            pltpu.VMEM((3, FEED_ROWS, D), BF16),
+            pltpu.VMEM((3, FEED_ROWS, D), BF16),
             pltpu.VMEM((SLOTS * HEAD_DIM, D), BF16),
             pltpu.VMEM((4, 48, D), BF16),
-            dma((5, CHIPS)), dma((5, CHIPS)), dma((2, 4)), dma((2, 4)), dma((2, 4)),
-            dma((3, 4)), dma((3, 4)),
+            dma(2, 6), dma(2, 6), dma(2, 6), dma(2, 6), dma(4), dma(4), dma(4),
+            dma(5), dma(5), dma(5), dma(4, 4), dma(4, 4), dma(2, 3), dma(2, 3),
         ],
         compiler_params=params(3, 63),
         name="feed",
-    )(middle, cot, halves, up_bias, gain, shift, down_bias, out_w, mixed)
+    )(middle, cots, halves, vecs, out_w, mixed)
 
 
 def back_kernel(
-    x, grad_mid, dq, dk, dv, hid, whole, gain,
-    grad_x, g_qkv, sums, head_sums,
-    joint, full, land, land_k, land_v, part, land_h,
-    send, recv, kv_send, kv_recv, g_send, g_recv,
+    x, grad_mid, dq, dk, dv, hid, whole, vecs, share, g_out, sums, up_sum,
+    grad_x, up_out, down_out, qkv_out, o_out, totals,
+    joint, full, land, land_k, land_v, part, sum_land, g_qkv, z_right, z_left, s_qkv,
+    s_out, zo_right, zo_left, own_qkv, own_out, all_feed, all_qkv, all_out, local, vec_land,
+    kv_send, kv_recv, g_send, g_recv, s_send, s_recv, a_send, a_recv, z_send, z_recv, t_send, t_recv, v_send, v_recv,
 ):
-    t, p, z = position()
-    greet(t, p, z)
+    e = Place()
+    t, p, z = (e.t, e.p, e.z)
+    e.greet()
     swaps = []
     for k in range(CHIPS):
-        other = (t + CHIPS - k) % CHIPS * 2 + 1 - p
-        mine = (t + CHIPS - k) % CHIPS
+        chip = e.flip(1 - k // 2, 1 - k % 2)
         for j, (ref, dst) in enumerate(((dk, land_k), (dv, land_v))):
             swaps.append(
-                to_twin(ref.at[other], dst.at[mine], kv_send.at[j, k], kv_recv.at[j, k], t, p, z)
+                remote(ref.at[chip * 2 + 1 - p], dst.at[chip], kv_send.at[j, k], kv_recv.at[j, k], e.twin())
             )
     for copy in swaps:
         copy.start()
+
+    def spread(number, own, everything, rows, cut):
+        return Gather(
+            e, own, lambda chip: everything.at[p, chip], rows, cut, a_send.at[number], a_recv.at[number]
+        )
+
+    def hand(number, own, everything, k):
+        chip = e.flip(k % 2, k // 2)
+        src = own if k == 0 else everything.at[p, chip]
+        return remote(
+            src, everything.at[p, chip], t_send.at[number, k], t_recv.at[number, k], e.twin()
+        )
+
+    def handed(number, own, everything):
+        for k in range(CHIPS):
+            chip = e.flip(k % 2, k // 2)
+            copy = remote(
+                own, everything.at[1 - p, chip], t_send.at[number, k], t_recv.at[number, k], e.twin()
+            )
+            copy.wait_recv()
+            copy.wait_send()
+
+    feeds = spread(0, share, all_feed, FEED_ROWS, 144)
+    feeds.start()
+    outs = ZScatter(e, g_out, s_out, zo_right, zo_left, z_send.at[0], z_recv.at[0])
+    outs.begin()
     normed, inverse = normalize(x[...].astype(F32))
+    local[...] = jnp.zeros_like(local)
+    head_q, head_v = (jnp.zeros((1, WIDE), F32), jnp.zeros((1, WIDE), F32))
     for copy in swaps:
         copy.wait()
-    head_sums[...] = jnp.zeros_like(head_sums)
-
-    def block(k, carry):
-        dst = (t + k) % CHIPS
-        mine = dst * 2 + p
-        joint[dst, :, :WIDE] = dq[dst]
-        joint[dst, :, WIDE : 2 * WIDE] = (dk[mine].astype(F32) + land_k[dst].astype(F32)).astype(BF16)
-        low_v = (dv[mine].astype(F32) + land_v[dst].astype(F32)).astype(BF16)
-        joint[dst, :, 2 * WIDE :] = low_v
-        head_sums[0:1] += jnp.sum(dq[dst].astype(F32), 0, keepdims=True)
-        head_sums[1:2] += jnp.sum(low_v.astype(F32), 0, keepdims=True)
-        part[dst] = cols_product(joint[dst], whole[...]).astype(BF16)
-
-        to_chip(part.at[dst], land_h.at[t], send.at[k], recv.at[k], t, p, z, k).start()
-        return carry
-
-    lax.fori_loop(1, CHIPS, block, 0)
-    joint[t, :, :WIDE] = dq[t]
-    joint[t, :, WIDE : 2 * WIDE] = (dk[t * 2 + p].astype(F32) + land_k[t].astype(F32)).astype(BF16)
-    low_v = (dv[t * 2 + p].astype(F32) + land_v[t].astype(F32)).astype(BF16)
-    joint[t, :, 2 * WIDE :] = low_v
-    head_sums[0:1] += jnp.sum(dq[t].astype(F32), 0, keepdims=True)
-    head_sums[1:2] += jnp.sum(low_v.astype(F32), 0, keepdims=True)
-    total = cols_product(joint[t], whole[...])
+    hand(0, share, all_feed, 0).start()
+    all_feed[p, t] = share[...]
+    for k in range(CHIPS):
+        mine = k * 2 + p
+        joint[k, :, :WIDE] = dq[k]
+        joint[k, :, WIDE : 2 * WIDE] = (dk[mine].astype(F32) + land_k[k].astype(F32)).astype(BF16)
+        low_v = (dv[mine].astype(F32) + land_v[k].astype(F32)).astype(BF16)
+        joint[k, :, 2 * WIDE :] = low_v
+        head_q = head_q + jnp.sum(dq[k].astype(F32), 0, keepdims=True)
+        head_v = head_v + jnp.sum(low_v.astype(F32), 0, keepdims=True)
+    outs.first()
 
     def stack(ref):
         return ref[...].reshape(CHIPS * ROWS, ref.shape[-1])
 
     full[...] = rows_product(stack(hid), stack(joint)).astype(BF16)
     swaps = [
-        to_twin(
-            full.at[rows16(i * 272 + (1 - p) * 128, 144)],
-            land.at[i],
-            g_send.at[i],
-            g_recv.at[i],
-            t,
-            p,
-            z,
+        remote(
+            full.at[rows16(i * 272 + (1 - p) * TILE, 144)], land.at[i], g_send.at[i], g_recv.at[i], e.twin()
         )
         for i in range(4)
     ]
     for copy in swaps:
         copy.start()
+    feeds.forward()
+    outs.second()
+    summed = Scatter(e, part, sum_land, s_send, s_recv)
+
+    def block(k, carry):
+        dest = e.flip(1 - k // 2, 1 - k % 2)
+        part[dest] = cols_product(joint[dest], whole[...]).astype(BF16)
+
+        @pl.when(k == 0)
+        def _():
+            summed.far_ready()
+
+        @pl.when(k == 1)
+        def _():
+            summed.x_ready()
+
+        @pl.when(k == 2)
+        def _():
+            summed.y_ready()
+
+        return carry
+
+    lax.fori_loop(0, 1, block, 0)
     for copy in swaps:
         copy.wait()
     for i in range(4):
-        own = full[rows16(i * 272 + p * 128, 144)].astype(F32)
+        own = full[rows16(i * 272 + p * TILE, 144)].astype(F32)
         g_qkv[i] = (own + land[i].astype(F32)).astype(BF16)
-    for k in range(1, CHIPS):
-        dst = (t + k) % CHIPS
-        to_chip(part.at[dst], land_h.at[t], send.at[k], recv.at[k], t, p, z, k).wait()
-        total = total + land_h[(t + CHIPS - k) % CHIPS].astype(F32)
-    grad_x[...] = grad_mid[...] + norm_back(total, normed, inverse, gain[...])
-    sums[0:1] = jnp.sum(total * normed, 0, keepdims=True)
-    sums[1:2] = jnp.sum(total, 0, keepdims=True)
-    sums[2:8] = jnp.zeros((6, D), F32)
-
-
-def back(x, grad_mid, dq, dk, dv, hid, whole, gain):
-    dma = pltpu.SemaphoreType.DMA
+    weights = ZScatter(e, g_qkv, s_qkv, z_right, z_left, z_send.at[1], z_recv.at[1])
+    weights.begin()
+    lax.fori_loop(1, CHIPS - 1, block, 0)
+    outs.last(own_out)
+    rows = cols_product(joint[t], whole[...])
+    weights.first()
+    feeds.have_x()
+    feeds.have_y()
+    hand(0, share, all_feed, 1).start()
+    hand(0, share, all_feed, 2).start()
+    feeds.have_far()
+    hand(0, share, all_feed, 3).start()
+    others = spread(1, own_out, all_out, 48, 32)
+    others.start()
+    all_out[p, t] = own_out[...]
+    hand(1, own_out, all_out, 0).start()
+    summed.relay()
+    weights.second()
+    total = rows + summed.total()
+    grad_x[...] = grad_mid[...] + norm_back(total, normed, inverse, vecs[GAIN_1 : GAIN_1 + 1])
+    local[:4] = sums[:4]
+    local[4:5] = jnp.sum(total * normed, 0, keepdims=True)
+    local[5:6] = jnp.sum(total, 0, keepdims=True)
+    local[pl.ds(8 + t, 1), :] = up_sum[...]
+    local[pl.ds(12 + t, 1), :WIDE] = head_q
+    local[pl.ds(12 + t, 1), WIDE : 2 * WIDE] = head_v
+    twin = remote(local, vec_land.at[0], v_send.at[0], v_recv.at[0], e.twin())
+    twin.start()
+    others.forward()
+    others.have_x()
+    others.have_y()
+    hand(1, own_out, all_out, 1).start()
+    hand(1, own_out, all_out, 2).start()
+    others.have_far()
+    hand(1, own_out, all_out, 3).start()
+    twin.wait()
+    totals[...] = local[...] + vec_land[0]
+    planes = [
+        remote(totals, vec_land.at[k], v_send.at[k], v_recv.at[k], e.plane(k)) for k in range(1, 4)
+    ]
+    for copy in planes:
+        copy.start()
+    weights.last(own_qkv)
+    qkvs = spread(2, own_qkv, all_qkv, 144, 80)
+    qkvs.start()
+    hand(2, own_qkv, all_qkv, 0).start()
+    all_qkv[p, t] = own_qkv[...]
+    for copy in planes:
+        copy.wait()
+    local[...] = totals[...] + vec_land[1] + vec_land[2] + vec_land[3]
+    chips = [
+        remote(local, vec_land.at[3 + k], v_send.at[3 + k], v_recv.at[3 + k], e.chip(chip))
+        for k, chip in ((1, e.tx), (2, e.ty), (3, e.td))
+    ]
+    for copy in chips:
+        copy.start()
+
+    handed(0, share, all_feed)
+    for s in range(CHIPS):
+        for q in range(2):
+            rows = slice(q * TILE, q * TILE + 144)
+            for i in range(4):
+                column = D * i + HEAD_DIM * (i % 2) + 256 * s
+                up_out[rows, column : column + 256] = all_feed[q, s, :144, 256 * i : 256 * (i + 1)].astype(F32)
+            down_out[rows16(z % 2 * 64 + 256 * s + TILE * q, TILE)] = all_feed[q, s, 144:272].astype(F32)
+    for q in range(2):
+        rows = slice(q * TILE, q * TILE + 144)
+        for s in range(0, CHIPS, 2):
+            pair = [all_feed[q, s + i, :144, 1024:].astype(F32) for i in range(2)]
+            column = D * s + 1024
+            up_out[rows, column : column + TILE] = jnp.concatenate(pair, 1)
+        down_out[rows16((1 - z % 2) * 1024 + 32 * q, 32)] = all_feed[q, z, 272:].astype(F32)
+
+    handed(1, own_out, all_out)
+    ahead = (CHIPS - z) % CHIPS * 16
+    for s in range(CHIPS - 1):
+        o_out[rows16(ahead + HEAD_DIM * s, 48)] = all_out[0, s].astype(F32)
+        o_out[rows16(ahead + HEAD_DIM * s + 32, 32)] = all_out[1, s, :32].astype(F32)
+    for u in range(SLOTS):
+        q, first = ((0, 16 * u) if u < 3 else (1, 16 * u - 32))
+        strip = all_out[q, CHIPS - 1, first : first + 16].astype(F32)
+
+        @pl.when(16 * u < ahead)
+        def _():
+            o_out[16 * u : 16 * u + 16] = strip
+
+        @pl.when(16 * u >= ahead)
+        def _():
+            o_out[192 + 16 * u : 208 + 16 * u] = strip
+
+    qkvs.forward()
+    qkvs.have_x()
+    qkvs.have_y()
+    hand(2, own_qkv, all_qkv, 1).start()
+    hand(2, own_qkv, all_qkv, 2).start()
+    qkvs.have_far()
+    hand(2, own_qkv, all_qkv, 3).start()
+    for copy in chips:
+        copy.wait()
+    totals[...] = local[...] + vec_land[4] + vec_land[5] + vec_land[6]
+    handed(2, own_qkv, all_qkv)
+    source = {}
+    for s, heads in enumerate(HEAD_TABLE):
+        for slot, head in enumerate(heads):
+            if head >= 0:
+                for a in range(3):
+                    source[a * HEADS + head] = (s, a * WIDE + slot * HEAD_DIM)
+    for q in range(2):
+        rows = slice(q * TILE, q * TILE + 144)
+
+        def piece(g, side):
+            s, column = source[g]
+            tile = all_qkv[q, s, :, column // TILE * TILE : column // TILE * TILE + TILE].astype(F32)
+            return tile if column % TILE // HEAD_DIM == side else pltpu.roll(tile, HEAD_DIM, 1)
+
+        left = lax.broadcasted_iota(jnp.int32, (144, TILE), 1) < HEAD_DIM
+        for g in range(0, 3 * HEADS - 1, 2):
+            column = g * HEAD_DIM
+            qkv_out[rows, column : column + TILE] = jnp.where(left, piece(g, 0), piece(g + 1, 1))
+        column = (3 * HEADS - 1) * HEAD_DIM
+        qkv_out[rows, column : column + HEAD_DIM] = piece(3 * HEADS - 1, 0)[:, :HEAD_DIM]
+    for user in (feeds, others, qkvs, summed):
+        user.sent()
+
+
+def back(x, grad_mid, dq, dk, dv, hid, whole, vecs, share, g_out, sums, up_sum):
     heads = pltpu.VMEM((CHIPS, ROWS, WIDE), BF16)
-    blocks = pltpu.VMEM((CHIPS, ROWS, D), BF16)
+    qkv, out = ((144, 3 * WIDE), (48, D))
+
+    def many(count, shape):
+        return pltpu.VMEM((count, *shape), BF16)
+
     return pl.pallas_call(
         back_kernel,
         out_shape=(
             jax.ShapeDtypeStruct((ROWS, D), F32),
-            jax.ShapeDtypeStruct((4, 144, 3 * WIDE), BF16),
-            jax.ShapeDtypeStruct((8, D), F32),
-            jax.ShapeDtypeStruct((8, WIDE), F32),
+            jax.ShapeDtypeStruct((D // 4, 4 * D), F32),
+            jax.ShapeDtypeStruct((D, D), F32),
+            jax.ShapeDtypeStruct((D // 4, 3 * D), F32),
+            jax.ShapeDtypeStruct((D // 4, D), F32),
+            jax.ShapeDtypeStruct((16, D), F32),
         ),
-        in_specs=vmem(8),
-        out_specs=tuple(vmem(4)),
+        in_specs=vmem(12),
+        out_specs=tuple(vmem(6)),
         scratch_shapes=[
             pltpu.VMEM((CHIPS, ROWS, 3 * WIDE), BF16),
             pltpu.VMEM((D, 3 * WIDE), BF16),
-            pltpu.VMEM((4, 144, 3 * WIDE), BF16),
-            heads, heads, blocks, blocks,
-            dma((CHIPS,)), dma((CHIPS,)), dma((2, CHIPS)), dma((2, CHIPS)), dma((4,)), dma((4,)),
+            many(4, qkv),
+            heads, heads,
+            pltpu.VMEM((CHIPS, ROWS, D), BF16),
+            pltpu.VMEM((6, HALF, D), BF16),
+            many(4, qkv), many(3, qkv), many(3, qkv), many(4, qkv),
+            many(4, out), many(3, out), many(3, out),
+            pltpu.VMEM(qkv, BF16), pltpu.VMEM(out, BF16),
+            pltpu.VMEM((2, CHIPS, FEED_ROWS, D), BF16),
+            pltpu.VMEM((2, CHIPS, *qkv), BF16),
+            pltpu.VMEM((2, CHIPS, *out), BF16),
+            pltpu.VMEM((16, D), F32),
+            pltpu.VMEM((7, 16, D), F32),
+            dma(2, CHIPS), dma(2, CHIPS), dma(4), dma(4), dma(6), dma(6), dma(3, 6), dma(3, 6),
+            dma(2, 2, 3), dma(2, 2, 3), dma(3, 4), dma(3, 4), dma(7), dma(7),
         ],
-        compiler_params=params(4),
+        compiler_params=params(4, 63),
         name="back",
-    )(x, grad_mid, dq, dk, dv, hid, whole, gain)
-
-
-def shares(array):
-    return lax.psum_scatter(array.reshape((-1, array.shape[-1])), "wsh", scatter_dimension=0, tiled=True)
-
-
-def joined(pieces, keep):
-    pairs = pieces.reshape(CHIPS, 2, keep, pieces.shape[-1])
-    return jnp.concatenate([pairs[:, 0], pairs[:, 1, 16:]], axis=1)
+    )(x, grad_mid, dq, dk, dv, hid, whole, vecs, share, g_out, sums, up_sum)
 
 
 def plane_device(
@@ -1105,19 +1528,13 @@
     table = jnp.asarray(HEAD_TABLE, jnp.int32)
     select = columns_of(lax.dynamic_index_in_dim(table, t, 0, keepdims=False))
 
-    vectors = jnp.stack(
-        [
-            b_query, b_value, b_out, b_down, ln1_gain, ln1_bias, ln2_gain, ln2_bias,
-            lax.dynamic_slice_in_dim(b_up, t * shard, shard),
-        ]
-    )
-    vectors = lax.all_gather(vectors, "wsh", axis=1, tiled=True)
-    head_bias = jnp.dot(vectors[:2], select, preferred_element_type=F32)
-    vectors = vectors.astype(F32)
-    bias_q, bias_v = (head_bias[0:1], head_bias[1:2])
-    bias_o, bias_d, gain_1, shift_1, gain_2, shift_2, bias_u = [
-        vectors[i : i + 1] for i in range(2, 9)
-    ]
+    more = 1024 * (1 - z % 2)
+    biases = jnp.stack([b_query, b_value, b_out, b_down, ln1_gain, ln1_bias, ln2_gain, ln2_bias])
+    vec_in = lax.dynamic_update_slice(jnp.zeros((16, D), BF16), biases, (jnp.int32(0), z * shard))
+    first = lax.dynamic_slice_in_dim(b_up, 64 * (z % 2) + 256 * t, 256)
+    vec_in = lax.dynamic_update_slice(vec_in, first[None], (jnp.int32(B_UP), 256 * z))
+    last = jnp.where(z == t, lax.dynamic_slice_in_dim(b_up, more, 64), jnp.zeros((64,), BF16))
+    vec_in = lax.dynamic_update_slice(vec_in, last[None], (jnp.int32(B_UP), jnp.int32(1024)))
 
     qkv_rows = lax.dynamic_slice_in_dim(w_qkv, p * 128, 144, 0)
     qkv_half = jnp.concatenate(
@@ -1127,74 +1544,61 @@
         ],
         axis=1,
     ).astype(BF16)
-    qkv_half = lax.all_gather(qkv_half, "wsh", axis=0)
-
-    ahead = jnp.asarray((0, 48, 32, 16), jnp.int32)[z]
+
+    ahead = (CHIPS - z) % CHIPS * 16
     i = p * 32 + integers(48)
     early = jnp.where(i < HEAD_DIM, ahead + HEAD_DIM * t + i, -1)
     late = jnp.where(i < ahead, i, 192 + i)
     taken = jnp.where(t < CHIPS - 1, early, late)
     pick = (taken[:, None] == integers(shard)[None, :]).astype(BF16)
     out_half = jnp.dot(pick, w_out, preferred_element_type=F32).astype(BF16)
-    out_half = lax.all_gather(out_half, "wsh", axis=0)
+
+    q, k, v, hid, cots, whole, out_w, vecs = project(x, cot, qkv_half, out_half, vec_in, select)
 
     up_rows = lax.dynamic_slice_in_dim(w_up, p * 128, 144, 0)
     up_half = jnp.concatenate(
-        [lax.dynamic_slice_in_dim(up_rows, i * D + t * shard, shard, 1) for i in range(4)], axis=1
-    )
-    down_half = lax.dynamic_slice_in_dim(w_down, t * shard + p * 128, 144, 0)
-    halves = lax.all_gather(jnp.concatenate([up_half, down_half]), "wsh", axis=0)
-
-    q, k, v, hid, whole = project(x, qkv_half, gain_1, shift_1, bias_q, bias_v)
+        [
+            lax.dynamic_slice_in_dim(up_rows, i * D + 64 * (i % 2) + t * 256, 256, 1)
+            for i in range(4)
+        ]
+        + [lax.dynamic_slice_in_dim(up_rows, D * t + 1024 * (1 - t % 2), 64, 1)],
+        axis=1,
+    )
+    down_half = lax.dynamic_slice_in_dim(w_down, 64 * (z % 2) + 256 * t + p * 128, 128, 0)
+    down_more = lax.dynamic_slice_in_dim(w_down, more + p * 32, 32, 0)
+    halves = jnp.concatenate([up_half, down_half, down_more])
+    halves, q = lax.optimization_barrier((halves, q))
+    halves = lax.all_gather(halves, "wsh", axis=0)
+
     mixed, lse = attend(lengths, parity, q, k, v)
-    middle, out_w = out_project(x, mixed, out_half, bias_o)
-    output, grad_mid, grad_heads, g_out, g_feed, sums, up_sum = feed(
-        middle, cot, halves, bias_u, gain_2, shift_2, bias_d, out_w, mixed
-    )
-    feed_all = lax.all_gather(shares(g_feed), "ctx", axis=0)
-    out_all = lax.all_gather(shares(g_out), "ctx", axis=0)
+    middle = out_project(x, mixed, out_w, vecs)
+    output, grad_mid, grad_heads, g_out, share, sums, up_sum = feed(
+        middle, cots, halves, vecs, out_w, mixed
+    )
     dq, dk, dv = attend_back(lengths, parity, q, k, v, mixed, grad_heads, lse)
-    grad_x, g_qkv, sums_1, head_sums = back(x, grad_mid, dq, dk, dv, hid, whole, gain_1)
-    qkv_all = lax.all_gather(shares(g_qkv), "ctx", axis=0)
-
-    up_all = joined(feed_all[:, :144], 144)
-    grad_up = jnp.transpose(up_all.reshape(CHIPS, shard, 4, shard), (1, 2, 0, 3))
-    grad_up = grad_up.reshape(shard, 4 * D).astype(F32)
-    grad_down = joined(feed_all[:, 144:], 144).reshape(D, D).astype(F32)
-    row = integers(shard)
-    inner = row - ahead
-    source = jnp.where(
-        row < ahead,
-        240 + row,
-        jnp.where(inner < 192, inner // HEAD_DIM * 80 + inner % HEAD_DIM, 48 + row),
-    )
-    place = (source[:, None] == integers(320)[None, :]).astype(BF16)
-    grad_out = jnp.dot(place, joined(out_all, 48).reshape(320, D), preferred_element_type=F32)
-    selects = jnp.stack([columns_of(table[i]) for i in range(CHIPS)])
-    grad_qkv = jnp.concatenate(
-        [
-            lax.dot_general(
-                part, selects, (((0, 2), (0, 2)), ((), ())), preferred_element_type=F32
-            )
-            for part in jnp.split(joined(qkv_all, 144), 3, axis=2)
-        ],
-        axis=1,
-    )
-
-    head_vectors = lax.dot_general(
-        head_sums[:2],
-        select.astype(F32),
-        (((1,), (1,)), ((), ())),
-        precision=lax.Precision.HIGHEST,
-        preferred_element_type=F32,
-    )
-    ups = lax.dynamic_update_slice(
-        jnp.zeros((4, D), F32), up_sum.reshape(4, shard), (jnp.int32(0), t * shard)
-    )
-    totals = jnp.concatenate([sums[:4], sums_1[:2], head_vectors, ups])
-    totals = lax.psum(totals, ("ctx", "wsh"))
-    mine = lax.dynamic_slice_in_dim(totals, z * shard, shard, 1)
-    grad_b_up = lax.dynamic_index_in_dim(totals, 8 + z, 0, keepdims=False)
+    grad_x, grad_up, grad_down, grad_qkv, grad_out, totals = back(
+        x, grad_mid, dq, dk, dv, hid, whole, vecs, share, g_out, sums, up_sum
+    )
+
+    place = {}
+    for s, heads in enumerate(HEAD_TABLE):
+        for slot, head in enumerate(heads):
+            place[head] = (12 + s, slot * HEAD_DIM)
+
+    def head_vector(first):
+        pieces = []
+        for head in range(HEADS):
+            row, column = place[head]
+            pieces.append(totals[row, first + column : first + column + HEAD_DIM])
+        return jnp.concatenate(pieces)
+
+    vectors = jnp.stack([*(totals[i] for i in range(6)), head_vector(0), head_vector(WIDE)])
+    mine = lax.dynamic_slice_in_dim(vectors, z * shard, shard, 1)
+    ups = lax.dynamic_slice_in_dim(totals[8:12], z * 256, 256, 1).reshape(D - 64)
+    extra = lax.dynamic_index_in_dim(totals[8:12, 1024:], z, 0, keepdims=False)
+    grad_b_up = jnp.where(
+        z % 2 == 0, jnp.concatenate([ups, extra]), jnp.concatenate([extra, ups])
+    )
     return (
         output[None], grad_x[None],
         mine[4], mine[5], grad_qkv, mine[6], mine[7], grad_out, mine[0],

time: 644 us -> 418 us (0.65)
  waiting for transfers between devices: 104 us -> 0.04 us
  blocking collectives: 88.4 us -> 0 us
  local copies, waits for them, and re-layouts: 66.9 us -> 45.2 us
  matrix products: 13.6 us -> 5.57 us
  other arithmetic: 12.1 us -> 4.47 us
    reduce_scatter x3 -> x0, waiting for transfers between devices: 82.3 us -> none  [shares(): lax.psum_scatter(array.reshape((-1, array.shape[-1])), 'wsh', scatter_dim...]
    all_gather x3 -> x0, blocking collectives: 47.6 us -> none  [the longest x1 20.5 us: plane_device(): out_half = lax.all_gather(out_half, 'wsh', axis=0)]
    pallas_call x1, Pallas kernels: 143 us -> 100 us  [feed(): pl.pallas_call(feed_kernel, out_shape=(jax.ShapeDtypeStruct((ROWS, D), BF...]
    psum x1 -> x0, blocking collectives: 40.8 us -> none  [plane_device(): totals = lax.psum(totals, ('ctx', 'wsh'))]
    pallas_call x1, Pallas kernels: 46.5 us -> 85.3 us  [back(): pl.pallas_call(back_kernel, out_shape=(jax.ShapeDtypeStruct((ROWS, D), F3...]
    all_gather x4 -> x1, waiting for transfers between devices: 20.1 us -> 0.02 us  [plane_device(): halves = lax.all_gather(halves, 'wsh', axis=0)]
    convert_element_type x2 -> x0, local copies, waits for them, and re-layouts: 15.4 us -> none  [plane_device(): grad_up = grad_up.reshape(shard, 4 * D).astype(F32)]
    unnamed x79 -> x58, local copies, waits for them, and re-layouts: 14.4 us -> 29 us
  transfers between devices with their start and end apart: 7 -> 1, of which waited for: 3 -> 0; matrix products, arithmetic and copies ran while one was open for 5% -> 0% of each run, Pallas kernels for 18% -> 16%
where the time goes in v2:
time: 418 us; the launch traced here: 411 us
  Pallas kernels  341 us (82%)
  local copies, waits for them, and re-layouts  45.2 us (11%)
  between operations  14.9 us (4%)
  matrix products  5.57 us (1%)
  other arithmetic  4.47 us (1%)
    pallas_call x1, Pallas kernels, feed(): pl.pallas_call(feed_kernel, out_shape=(jax.ShapeDtypeStruct((ROWS, D), BF...  100 us
    pallas_call x1, Pallas kernels, back(): pl.pallas_call(back_kernel, out_shape=(jax.ShapeDtypeStruct((ROWS, D), F3...  85.3 us
    pallas_call x1, Pallas kernels, project(): pl.pallas_call(project_kernel, out_shape=(blocks, keys, keys, rows, rows,...  56.1 us
    pallas_call x1, Pallas kernels, attend_back(): pl.pallas_call(attend_back_kernel, out_shape=(jax.ShapeDtypeStruct((CHIPS...  33.9 us
    pallas_call x1, Pallas kernels, attend(): pl.pallas_call(attend_kernel, out_shape=(jax.ShapeDtypeStruct((CHIPS, ROW...  33 us
    pallas_call x1, Pallas kernels, out_project(): pl.pallas_call(out_kernel, out_shape=jax.ShapeDtypeStruct((ROWS, D), F32)...  32.1 us
    unnamed x58, local copies, waits for them, and re-layouts  29 us
  transfers between devices with their start and end apart: 1, of which 0 were waited for; matrix products, arithmetic and copies ran while one was open for 0% of the time, Pallas kernels for 16%

profile of v2, /device:TPU:0, one launch (start us, length us, event | category | flops | bytes accessed | tf_op | source)
XLA Modules:
  0.0 410.8 jit_solution(3224846893863564419)
XLA Ops:
  14.5 1.2 fusion.select
  15.7 1.5 fusion.4
  17.3 1.5 fusion.6
  18.8 1.6 fusion.5
  22.3 1.1 copy.32
  23.3 1.1 copy.33
  33.9 56.1 %project.1 = (bf16[4,256,384]{2,1,0:T(8,128)(2,1)}, bf16[8,256,384]{2,1,0:T(8,128)(2,1)}, bf16[8,256,384]{2,1,0:T(8,128)(2,1)}, bf16[4,256,1088]{2,1,0:T(8,128)(...) custom-call(bf16[256,1088]{1,0:T(8,128)(2,1)} %bitcast.87, ...), custom_call_target="tpu_custom_call" | custom-call | tf_op jit(solution)/shard_map/project/pallas_call | solution.py:731
  90.0 1.4 copy-done.6
  91.4 1.4 copy-done.7
  92.8 1.1 copy-done.8
  94.0 33.0 %attend.1 = (bf16[4,256,384]{2,1,0:T(8,128)(2,1)S(1)}, f32[3,8,256]{2,1,0:T(8,128)S(1)}) custom-call(s32[5]{0:T(128)S(1)} %bitcast.85, s32[1]{0:T(128)} %bitcast.2.parity, bf16[4,256,384]{2,1,0:T(8,128)(2,1)S(1)} %copy-done.8, bf16[8,256,384]{2,1,0:T(8,128)(2,1)S(1)} %copy-done.6, bf16[8,256,384]{2,1,0:T(8,128)(2,1)S(1)} %copy-done.7), custom_call_target="tpu_custom_call" | custom-call | flops 4000000000 | bytes 5000000 | tf_op jit(solution)/shard_map/attend/pallas_call | solution.py:852
  127.8 32.1 %out_project.1.middle = f32[256,1088]{1,0:T(8,128)} custom-call(bf16[256,1088]{1,0:T(8,128)(2,1)} %bitcast.88, bf16[4,256,384]{2,1,0:T(8,128)(2,1)} %copy-done.2, bf16[384,1088]{1,0:T(8,128)(2,1)} %get-tuple-element.48.whole.out_w, f32[16,1088]{1,0:T(8,128)} %get-tuple-element.49.vecs), custom_call_target="tpu_custom_call" | custom-call | tf_op jit(solution)/shard_map/out_project/pallas_call | solution.py:1003
  160.0 100.2 %feed.1 = (bf16[256,1088]{1,0:T(8,128)(2,1)}, f32[256,1088]{1,0:T(8,128)}, bf16[4,256,384]{2,1,0:T(8,128)(2,1)}, bf16[4,48,1088]{2,1,0:T(8,128)(2,1)}, bf16[304,...) custom-call(f32[256,1088]{1,0:T(8,128)} %out_project.1.middle, ...), custom_call_target="tpu_custom_call" | custom-call | tf_op jit(solution)/shard_map/feed/pallas_call | solution.py:1208
  260.3 1.1 copy-done.9
  261.4 1.1 copy-done.10
  262.5 33.9 %attend_back.1 = (bf16[4,256,384]{2,1,0:T(8,128)(2,1)S(1)}, bf16[8,256,384]{2,1,0:T(8,128)(2,1)S(1)}, bf16[8,256,384]{2,1,0:T(8,128)(2,1)}) custom-call(s32[5]{0:T(128)S(1)} %bitcast.86, s32[1]{0:T(128)} %bitcast.2.parity, bf16[4,256,384]{2,1,0:T(8,128)(2,1)S(1)} %copy-done.9, bf16[8,256,384]{2,1,0:T(8,128)(2,1)} %get-tuple-element.45.k, ...), custom_call_target="tpu_custom_call" | custom-call | flops 10000000000 | bytes 9000000 | tf_op jit(solution)/shard_map/attend_back/pallas_call | solution.py:945
  296.4 1.1 copy-done.4
  298.4 85.3 %back.1 = (f32[256,1088]{1,0:T(8,128)}, f32[272,4352]{1,0:T(8,128)}, f32[1088,1088]{1,0:T(8,128)}, f32[272,3264]{1,0:T(8,128)}, f32[272,1088]{1,0:T(8,128)}, /*index=5*/f32[16,1088]{1,0:T(8,128)}) custom-call(bf16[256,1088]{1,0:T(8,128)(2,1)} %bitcast.89, f32[256,1088]{1,0:T(8,128)} %get-tuple-element.53.grad_mid, bf16[4,256,384]{2,1,0:T(8,128)(2,1)} %copy-done.5, ...), custom_call_target="tpu_custom_call" | custom-call | tf_op jit(solution)/shard_map/back/pallas_call | solution.py:1476
  384.5 1.0 slice_bitcast_fusion.19
  385.5 1.1 slice_bitcast_fusion
  389.2 1.3 copy.35
  392.2 4.2 %copy.48 = f32[272,3264]{1,0:T(8,128)} copy(f32[272,3264]{1,0:T(8,128)} %get-tuple-element.147) | data formatting | bytes 7102464
  397.5 2.4 copy.50
  401.1 2.3 copy.51
  (90 shorter events, 27.7 us)
Async XLA Ops:
  7.2 19.0 %copy-start = (bf16[272,1088]{1,0:T(8,128)(2,1)S(1)}, bf16[272,1088]{1,0:T(8,128)(2,1)}, u32[]{:S(2)}) copy-start(bf16[272,1088]{1,0:T(8,128)(2,1)} %param.25) | copy-start | bytes 1775620
  7.2 152.8 %all-gather.3.cloned.1.call-start = ((), (), s32[]{:S(2)}) async-start(), calls=%async_computation | async-start | bytes 3502080 | tf_op jit(solution)/shard_map/all_gather | solution.py:1571
  15.7 6.5 %copy-start.15 = (bf16[1,256,1088]{1,2,0:T(8,128)(2,1)S(1)}, bf16[1,256,1088]{1,2,0:T(8,128)(2,1)}, u32[]{:S(2)}) copy-start(bf16[1,256,1088]{1,2,0:T(8,128)(2,1)} %param.17) | copy-start | bytes 1671172
  17.2 6.1 %copy-start.16 = (bf16[1,256,1088]{1,2,0:T(8,128)(2,1)S(1)}, bf16[1,256,1088]{1,2,0:T(8,128)(2,1)}, u32[]{:S(2)}) copy-start(bf16[1,256,1088]{1,2,0:T(8,128)(2,1)} %param.19) | copy-start | bytes 1671172
  26.2 7.7 %copy-start.17 = (bf16[16,1088]{1,0:T(8,128)(2,1)}, bf16[16,1088]{1,0:T(8,128)(2,1)S(1)}, u32[]{:S(2)}) copy-start(bf16[16,1088]{1,0:T(8,128)(2,1)S(1)} %dynamic_update_slice.11.vec_in) | copy-start | bytes 104452
  33.9 56.1 %copy-start.11 = (s32[1,5]{1,0:T(1,128)S(1)}, s32[1,5]{1,0:T(1,128)}, u32[]{:S(2)}) copy-start(s32[1,5]{1,0:T(1,128)} %param.18) | copy-start | bytes 64
  90.0 1.4 copy-start.6
  91.4 1.4 copy-start.7
  92.8 1.1 copy-start.8
  127.0 0.9 copy-start.2
  160.0 100.3 %copy-start.3 = (bf16[4,256,384]{2,1,0:T(8,128)(2,1)S(1)}, bf16[4,256,384]{2,1,0:T(8,128)(2,1)}, u32[]{:S(2)}) copy-start(bf16[4,256,384]{2,1,0:T(8,128)(2,1)} %copy-done.2) | copy-start | bytes 2359300
  260.2 1.1 copy-start.9
  261.4 1.1 copy-start.10
  296.4 1.1 copy-start.4
  297.6 0.9 copy-start.5
  298.4 89.7 %copy-start.14 = (bf16[256,1088]{1,0:T(8,128)(2,1)S(1)}, bf16[256,1088]{1,0:T(8,128)(2,1)}, u32[]{:S(2)}) copy-start(bf16[256,1088]{1,0:T(8,128)(2,1)} %get-tuple-element.52) | copy-start | bytes 1671172
  383.7 5.5 %copy-start.13 = (f32[256,1088]{1,0:T(8,128)S(1)}, f32[256,1088]{1,0:T(8,128)}, u32[]{:S(2)}) copy-start(f32[256,1088]{1,0:T(8,128)} %get-tuple-element.65) | copy-start | bytes 3342340
  390.7 6.8 %slice-start.2 = ((s8[4734976]{0:T(1024)(128)(4,1)}), s8[4194304]{0:T(1024)(128)(4,1)S(1)}, s32[]{:S(2)}) async-start(s8[4734976]{0:T(1024)(128)(4,1)} %bitcast.92), calls=%async_computation.3 | async-start | bytes 8388608
  392.2 4.2 %copy-start.12 = (f32[272,1088]{1,0:T(8,128)S(1)}, f32[272,1088]{1,0:T(8,128)}, u32[]{:S(2)}) copy-start(f32[272,1088]{1,0:T(8,128)} %get-tuple-element.150) | copy-start | bytes 3551236
  392.2 5.3 %slice-start.3 = ((s8[4734976]{0:T(1024)(128)(4,1)}), s8[540672]{0:T(1024)(128)(4,1)S(1)}, s32[]{:S(2)}) async-start(s8[4734976]{0:T(1024)(128)(4,1)} %bitcast.92), calls=%async_computation.4 | async-start | bytes 1081344
  396.4 4.3 %slice-start = ((s8[5013504]{0:T(1024)(128)(4,1)}), s8[4194304]{0:T(1024)(128)(4,1)S(1)}, s32[]{:S(2)}) async-start(s8[5013504]{0:T(1024)(128)(4,1)} %bitcast.90), calls=%async_computation.1 | async-start | bytes 8388608
  397.5 3.7 slice-start.1
  401.1 2.3 copy-start.1
Sparse Core Ops, SparseCore 0:
  90.1 56.5 all-gather.2
